TPU v7x, 512 devices: a whole 4x4x16 slice. The times are simulated.
512 devices in a mesh: rows: 64 (over z, y), cols: 8 (over x, core).
Axes of the slice: x: 4, y: 4, z: 16, core: 2. Of those that a mesh axis runs over, the one named last changes fastest.
Arguments:
- sens_base: bfloat16 [524288, 1024], P('rows', 'cols'), may hold values from -0.14157282 to 0.14157282
- design_field: float32 [512, 1024], P('rows'), may hold values from -3 to 3
- gradient: bfloat16 [512, 1024], P('rows'), may hold values from -6 to 6
- tile_index: int32 [1024], P('cols'), may hold values from 0 to 31
- type_codes: int32 [1024], P('cols'), may hold values from 0 to 2
Outputs:
- r_panels: float32 [512, 1024], P(None, 'cols')
- multipliers: float32 [512], replicated
Inputs may be any that keep to these rules, and one draw needn't show every extreme that they name: `tile_index`: each constraint names one support tile.
All inputs are finite; a program needn't handle non-finite values.
Results may differ from a plain program's by a relative error of at most 0.0003.
The roundings to bfloat16 on the way count: a program that leaves them out, or rounds other values in their place, can miss the bound.
Values may be sent and summed in bfloat16 or wider, within the bound.
A program may use at most 64 MiB of HBM per device.

v0:
```python
import math

import jax
import jax.numpy as jnp
from jax import lax
from jax.sharding import PartitionSpec as P

TILE = 128
PW = 256


def padded_2(cells, sides, width):
    for axis, dim in sides:
        count = lax.axis_size(axis)
        ends = count - 1
        head = lax.slice_in_dim(cells, 0, width, axis=dim)
        tail = lax.slice_in_dim(cells, cells.shape[dim] - width, cells.shape[dim], axis=dim)
        cells = jnp.concatenate(
            [
                lax.ppermute(tail, axis, [(i, (i + 1) % count) for i in range(ends)]),
                cells,
                lax.ppermute(head, axis, [((i + 1) % count, i) for i in range(ends)]),
            ],
            axis=dim,
        )
    return cells


def assemble(base_cols, tile_cols, type_cols, stencils, cell_tile):
    kinds_all = jnp.arange(3, dtype=jnp.int32)
    chooser = (type_cols[None, :] == kinds_all[:, None]).astype(jnp.float32)
    picked = lax.dot_general(
        stencils,
        chooser,
        (((0,), (0,)), ((), ())),
        precision=lax.Precision.HIGHEST,
        preferred_element_type=jnp.float32,
    )
    inside = cell_tile[:, None] == tile_cols[None, :]
    total = base_cols.astype(jnp.float32) + jnp.where(inside, picked / TILE, 0.0)
    return total.astype(jnp.bfloat16)


def matmul(left, right):
    return jnp.dot(left, right, precision=lax.Precision.HIGHEST, preferred_element_type=jnp.float32)


def small_factor(matrix):
    order = matrix.shape[0]
    positions = jnp.arange(order, dtype=jnp.int32)

    def column_step(index_col, carry):
        working, lower = carry
        column = lax.dynamic_slice_in_dim(working, index_col, 1, 1)[:, 0]
        pivot = jnp.sqrt(lax.dynamic_slice_in_dim(column, index_col, 1, 0)[0])
        column = jnp.where(positions >= index_col, column / pivot, 0.0)
        lower = jnp.where(positions[None, :] == index_col, column[:, None], lower)
        working = working - column[:, None] * column[None, :]
        return (working, lower)

    return lax.fori_loop(0, order, column_step, (matrix, jnp.zeros_like(matrix)))[1]


def small_inverse(lower):
    order = lower.shape[0]
    positions = jnp.arange(order, dtype=jnp.int32)
    right = jnp.eye(order, dtype=jnp.float32)

    def row_step(index_row, carry):
        rest, solved = carry
        column = lax.dynamic_slice_in_dim(lower, index_row, 1, 1)[:, 0]
        pivot = lax.dynamic_slice_in_dim(column, index_row, 1, 0)[0]
        value = lax.dynamic_slice_in_dim(rest, index_row, 1, 0) / pivot
        solved = jnp.where(positions[:, None] == index_row, value, solved)
        below = jnp.where(positions > index_row, column, 0.0)
        rest = rest - below[:, None] * value
        return (rest, solved)

    return lax.fori_loop(0, order, row_step, (right, jnp.zeros_like(right)))[1]


def factor_lower(matrix):
    order = matrix.shape[0]
    width = math.gcd(order, 32)
    working = matrix
    lower = jnp.zeros_like(matrix)
    inverses = []
    for block_num in range(order // width):
        start = block_num * width
        diag_lower = small_factor(working[:width, :width])
        diag_inverse = small_inverse(diag_lower)
        inverses.append(diag_inverse)
        lower = lower.at[start : start + width, start : start + width].set(diag_lower)
        if start + width < order:
            panel = matmul(working[width:, :width], diag_inverse.T)
            lower = lower.at[start + width :, start : start + width].set(panel)
            working = working[width:, width:] - matmul(panel, panel.T)
    return (lower, inverses)


def solve_forward(lower, inverses, right):
    width = inverses[0].shape[0]
    solved = []
    for block_num in range(len(inverses)):
        start = block_num * width
        rest = right[start : start + width]
        if block_num > 0:
            rest = rest - matmul(
                lower[start : start + width, :start], jnp.concatenate(solved, axis=0)
            )
        solved.append(matmul(inverses[block_num], rest))
    return jnp.concatenate(solved, axis=0)


def solve_backward(lower, inverses, right):
    width = inverses[0].shape[0]
    order = lower.shape[0]
    solved = []
    for block_num in reversed(range(len(inverses))):
        start = block_num * width
        rest = right[start : start + width]
        if start + width < order:
            rest = rest - matmul(
                lower[start + width :, start : start + width].T, jnp.concatenate(solved, axis=0)
            )
        solved.insert(0, matmul(inverses[block_num].T, rest))
    return jnp.concatenate(solved, axis=0)


def shards(sens_base, design_field, gradient, tile_index, type_codes):
    rows_here = design_field.shape[0]
    grid_width = design_field.shape[1]
    cols_here = sens_base.shape[1]
    factored = 2 * PW
    padded = padded_2(design_field, (("rows", 0),), 1)
    padded = jnp.pad(padded, ((0, 0), (1, 1)))
    north_cells = padded[:-2, 1:-1]
    south_cells = padded[2:, 1:-1]
    west_cells = padded[1:-1, :-2]
    east_cells = padded[1:-1, 2:]
    laplace = 4.0 * design_field - (north_cells + south_cells + west_cells + east_cells)
    slope_x = 0.5 * (east_cells - west_cells)
    slope_y = 0.5 * (south_cells - north_cells)
    stencils = jnp.stack([laplace, slope_x, slope_y]).reshape(3, -1)
    row_glob = lax.axis_index("rows") * rows_here + jnp.arange(rows_here, dtype=jnp.int32)
    col_ids = jnp.arange(grid_width, dtype=jnp.int32) // TILE
    cell_tile = ((row_glob // TILE)[:, None] * (grid_width // TILE) + col_ids[None, :]).reshape(-1)
    local_jac = assemble(sens_base, tile_index, type_codes, stencils, cell_tile)
    grad_flat = gradient.reshape(-1)
    row_major = lax.all_to_all(local_jac, "cols", split_axis=0, concat_axis=1, tiled=True)
    row_piece = row_major.shape[0]
    grad_part = lax.dynamic_slice_in_dim(
        grad_flat, lax.axis_index("cols") * row_piece, row_piece, 0
    )
    leading = row_major[:, :factored]
    gram_block = lax.dot_general(
        leading, row_major, (((0,), (0,)), ((), ())), preferred_element_type=jnp.float32
    )
    projected = jnp.dot(grad_part, leading, preferred_element_type=jnp.float32)
    gram_block, projected = lax.psum((gram_block, projected), ("rows", "cols"))
    gram_head = gram_block[:, :factored]
    gram_own = lax.dynamic_slice_in_dim(
        gram_block, lax.axis_index("cols") * cols_here, cols_here, 1
    )
    lower_chol, inverses = factor_lower(gram_head)
    r_panels = solve_forward(lower_chol, inverses, gram_own)
    half_solved = solve_forward(lower_chol, inverses, projected[:, None])
    multipliers = solve_backward(lower_chol, inverses, half_solved)[:, 0]
    return (r_panels, multipliers)


def solution(mesh):
    placed = (P("rows", "cols"), P("rows", None), P("rows", None), P("cols"), P("cols"))
    return jax.shard_map(
        shards, mesh=mesh, in_specs=placed, out_specs=(P(None, "cols"), P()), check_vma=False
    )
```

profile of v0, /device:TPU:1, one launch (start us, length us, event | category | flops | bytes accessed | tf_op | source)
XLA Modules:
  0.0 2140.8 jit_solution(14819654451309352459)
XLA Ops:
  8.1 4.0 collective-permute-start
  13.5 2.9 collective-permute-done.1
  18.4 6.7 fusion.98
  25.0 2.9 copy.37
  27.9 34.2 %all_to_all.19 = bf16[8,1024,128]{1,2,0:T(8,128)(2,1)S(1)} all-to-all(bf16[8,1024,128]{1,2,0:T(8,128)(2,1)S(1)} %copy.37), channel_id=1, replica_groups=mesh['rows'=64,'cols'=8] {'cols'}, dimensions={0} | all-to-all | bytes 4194304 | tf_op jit(solution)/shard_map/all_to_all | solution.py:150
  63.4 2.6 fusion.161
  68.0 110.2 %psum.15 = f32[512]{0:T(512)S(1)} all-reduce(f32[512]{0:T(512)S(1)} %bitcast.1236), channel_id=1, replica_groups=mesh['rows'=64,'cols'=8] {'rows','cols'}, use_global_device_ids=true, to_apply=%region_65.66 | all-reduce | flops 512 | bytes 4096 | tf_op jit(solution)/shard_map/psum | solution.py:160
  178.3 367.6 %all-reduce.4.cloned.1.call-done = f32[512,1024]{1,0:T(8,128)} async-done(((f32[512,1024]{1,0:T(8,128)}), f32[512,1024]{1,0:T(8,128)}) %all-reduce.4.cloned.1.call-update) | async-done | bytes 2097168 | tf_op jit(solution)/shard_map/psum | solution.py:160
  546.7 45.5 %while.671 = (s32[]{:T(128)}, f32[32,32]{0,1:T(8,128)S(1)}, f32[32,32]{0,1:T(8,128)S(1)}, s32[]{:T(128)}, s32[]{:T(128)}, /*index=5*/s32[]{:T(128)}) while((s32[]{:T(128)}, f32[32,32]{0,1:T(8,128)S(1)}, f32[32,32]{0,1:T(8,128)S(1)}, s32[]{:T(128)}, s32[]{:T(128)}, /*index=5*/s32[]{:T(128)}) %tuple.1741), condition=%wide.region_2.3_spmd.clone.clone, body=%wide.region_1.2_spmd.clone.clone.sunk | while | flops 4292 | bytes 19003 | solution.py:61
  592.2 43.6 %while.672 = (s32[]{:T(128)}, f32[32,32]{1,0:T(8,128)S(1)}, f32[32,32]{1,0:T(8,128)S(1)}, f32[32,32]{0,1:T(8,128)S(1)}, s32[]{:T(128)}, /*index=5*/s32[]{:T(128)}, s32[]{:T(128)}) while((s32[]{:T(128)}, f32[32,32]{1,0:T(8,128)S(1)}, f32[32,32]{1,0:T(8,128)S(1)}, f32[32,32]{0,1:T(8,128)S(1)}, s32[]{:T(128)}, ...), condition=%wide.region_4.5_spmd.clone.clone, body=%wide.region_3.4_spmd.clone.clone.sunk | while | flops 4228 | bytes 18367 | solution.py:79
  637.2 2.3 convolution_subtract_fusion
  639.5 45.0 %while.673 = (s32[]{:T(128)}, f32[32,32]{0,1:T(8,128)S(1)}, f32[32,32]{0,1:T(8,128)S(1)}, s32[]{:T(128)}, s32[]{:T(128)}, /*index=5*/s32[]{:T(128)}) while((s32[]{:T(128)}, f32[32,32]{0,1:T(8,128)S(1)}, f32[32,32]{0,1:T(8,128)S(1)}, s32[]{:T(128)}, s32[]{:T(128)}, /*index=5*/s32[]{:T(128)}) %tuple.1747), condition=%wide.region_6.7_spmd.clone.clone, body=%wide.region_5.6_spmd.clone.clone.sunk | while | flops 4292 | bytes 19003 | solution.py:61
  684.6 43.6 %while.674 = (s32[]{:T(128)}, f32[32,32]{1,0:T(8,128)S(1)}, f32[32,32]{1,0:T(8,128)S(1)}, f32[32,32]{0,1:T(8,128)S(1)}, s32[]{:T(128)}, /*index=5*/s32[]{:T(128)}, s32[]{:T(128)}) while((s32[]{:T(128)}, f32[32,32]{1,0:T(8,128)S(1)}, f32[32,32]{1,0:T(8,128)S(1)}, f32[32,32]{0,1:T(8,128)S(1)}, s32[]{:T(128)}, ...), condition=%wide.region_8.9_spmd.clone.clone, body=%wide.region_7.8_spmd.clone.clone.sunk | while | flops 4228 | bytes 18367 | solution.py:79
  729.6 45.0 %while.675 = (s32[]{:T(128)}, f32[32,32]{0,1:T(8,128)S(1)}, f32[32,32]{0,1:T(8,128)S(1)}, s32[]{:T(128)}, s32[]{:T(128)}, /*index=5*/s32[]{:T(128)}) while((s32[]{:T(128)}, f32[32,32]{0,1:T(8,128)S(1)}, f32[32,32]{0,1:T(8,128)S(1)}, s32[]{:T(128)}, s32[]{:T(128)}, /*index=5*/s32[]{:T(128)}) %tuple.1753), condition=%wide.region_10.11_spmd.clone.clone, body=%wide.region_9.10_spmd.clone.clone.sunk | while | flops 4292 | bytes 19003 | solution.py:61
  774.6 43.6 %while.676 = (s32[]{:T(128)}, f32[32,32]{1,0:T(8,128)S(1)}, f32[32,32]{1,0:T(8,128)S(1)}, f32[32,32]{0,1:T(8,128)S(1)}, s32[]{:T(128)}, /*index=5*/s32[]{:T(128)}, s32[]{:T(128)}) while((s32[]{:T(128)}, f32[32,32]{1,0:T(8,128)S(1)}, f32[32,32]{1,0:T(8,128)S(1)}, f32[32,32]{0,1:T(8,128)S(1)}, s32[]{:T(128)}, ...), condition=%wide.region_12.13_spmd.clone.clone, body=%wide.region_11.12_spmd.clone.clone.sunk | while | flops 4228 | bytes 18367 | solution.py:79
  819.6 86.6 %while.677 = (s32[]{:T(128)}, f32[32,32]{0,1:T(8,128)S(1)}, f32[32,32]{0,1:T(8,128)}, s32[]{:T(128)}, s32[]{:T(128)}, /*index=5*/s32[]{:T(128)}) while((s32[]{:T(128)}, f32[32,32]{0,1:T(8,128)S(1)}, f32[32,32]{0,1:T(8,128)}, s32[]{:T(128)}, s32[]{:T(128)}, /*index=5*/s32[]{:T(128)}) %tuple.1759), condition=%wide.region_14.15_spmd.clone.clone, body=%wide.region_13.14_spmd.clone.clone.sunk | while | flops 4292 | bytes 19003 | solution.py:61
  825.7 1.4 select_select_fusion.70
  906.4 1.4 scatter.101
  907.8 2.1 scatter.104
  909.9 1.4 scatter.105
  911.3 2.1 scatter.106
  913.4 1.4 scatter.109
  914.8 2.1 scatter.110
  917.0 86.4 %while.678 = (s32[]{:T(128)}, f32[32,32]{1,0:T(8,128)S(1)}, f32[32,32]{1,0:T(8,128)S(1)}, f32[32,32]{0,1:T(8,128)}, s32[]{:T(128)}, /*index=5*/s32[]{:T(128)}, s32[]{:T(128)}) while((s32[]{:T(128)}, f32[32,32]{1,0:T(8,128)S(1)}, f32[32,32]{1,0:T(8,128)S(1)}, f32[32,32]{0,1:T(8,128)}, s32[]{:T(128)}, ...), condition=%wide.region_16.17_spmd.clone.clone, body=%wide.region_15.16_spmd.clone.clone.sunk | while | flops 4228 | bytes 18751 | solution.py:79
  1004.5 45.0 %while.679 = (s32[]{:T(128)}, f32[32,32]{0,1:T(8,128)S(1)}, f32[32,32]{0,1:T(8,128)S(1)}, s32[]{:T(128)}, s32[]{:T(128)}, /*index=5*/s32[]{:T(128)}) while((s32[]{:T(128)}, f32[32,32]{0,1:T(8,128)S(1)}, f32[32,32]{0,1:T(8,128)S(1)}, s32[]{:T(128)}, s32[]{:T(128)}, /*index=5*/s32[]{:T(128)}) %tuple.1856), condition=%wide.region_18.19_spmd.clone.clone, body=%wide.region_17.18_spmd.clone.clone.sunk | while | flops 4292 | bytes 19003 | solution.py:61
  1049.5 43.6 %while.680 = (s32[]{:T(128)}, f32[32,32]{1,0:T(8,128)S(1)}, f32[32,32]{1,0:T(8,128)S(1)}, f32[32,32]{0,1:T(8,128)S(1)}, s32[]{:T(128)}, /*index=5*/s32[]{:T(128)}, s32[]{:T(128)}) while((s32[]{:T(128)}, f32[32,32]{1,0:T(8,128)S(1)}, f32[32,32]{1,0:T(8,128)S(1)}, f32[32,32]{0,1:T(8,128)S(1)}, s32[]{:T(128)}, ...), condition=%wide.region_20.21_spmd.clone.clone, body=%wide.region_19.20_spmd.clone.clone.sunk | while | flops 4228 | bytes 18367 | solution.py:79
  1094.1 45.0 %while.681 = (s32[]{:T(128)}, f32[32,32]{0,1:T(8,128)S(1)}, f32[32,32]{0,1:T(8,128)S(1)}, s32[]{:T(128)}, s32[]{:T(128)}, /*index=5*/s32[]{:T(128)}) while((s32[]{:T(128)}, f32[32,32]{0,1:T(8,128)S(1)}, f32[32,32]{0,1:T(8,128)S(1)}, s32[]{:T(128)}, s32[]{:T(128)}, /*index=5*/s32[]{:T(128)}) %tuple.1855), condition=%wide.region_22.23_spmd.clone.clone, body=%wide.region_21.22_spmd.clone.clone.sunk | while | flops 4292 | bytes 19003 | solution.py:61
  1139.2 43.6 %while.682 = (s32[]{:T(128)}, f32[32,32]{1,0:T(8,128)S(1)}, f32[32,32]{1,0:T(8,128)S(1)}, f32[32,32]{0,1:T(8,128)S(1)}, s32[]{:T(128)}, /*index=5*/s32[]{:T(128)}, s32[]{:T(128)}) while((s32[]{:T(128)}, f32[32,32]{1,0:T(8,128)S(1)}, f32[32,32]{1,0:T(8,128)S(1)}, f32[32,32]{0,1:T(8,128)S(1)}, s32[]{:T(128)}, ...), condition=%wide.region_24.25_spmd.clone.clone, body=%wide.region_23.24_spmd.clone.clone.sunk | while | flops 4228 | bytes 18367 | solution.py:79
  1183.8 45.0 %while.683 = (s32[]{:T(128)}, f32[32,32]{0,1:T(8,128)S(1)}, f32[32,32]{0,1:T(8,128)S(1)}, s32[]{:T(128)}, s32[]{:T(128)}, /*index=5*/s32[]{:T(128)}) while((s32[]{:T(128)}, f32[32,32]{0,1:T(8,128)S(1)}, f32[32,32]{0,1:T(8,128)S(1)}, s32[]{:T(128)}, s32[]{:T(128)}, /*index=5*/s32[]{:T(128)}) %tuple.1854), condition=%wide.region_26.27_spmd.clone.clone, body=%wide.region_25.26_spmd.clone.clone.sunk | while | flops 4292 | bytes 19003 | solution.py:61
  1228.8 43.6 %while.684 = (s32[]{:T(128)}, f32[32,32]{1,0:T(8,128)S(1)}, f32[32,32]{1,0:T(8,128)S(1)}, f32[32,32]{0,1:T(8,128)S(1)}, s32[]{:T(128)}, /*index=5*/s32[]{:T(128)}, s32[]{:T(128)}) while((s32[]{:T(128)}, f32[32,32]{1,0:T(8,128)S(1)}, f32[32,32]{1,0:T(8,128)S(1)}, f32[32,32]{0,1:T(8,128)S(1)}, s32[]{:T(128)}, ...), condition=%wide.region_28.29_spmd.clone.clone, body=%wide.region_27.28_spmd.clone.clone.sunk | while | flops 4228 | bytes 18367 | solution.py:79
  1273.3 45.0 %while.685 = (s32[]{:T(128)}, f32[32,32]{0,1:T(8,128)S(1)}, f32[32,32]{0,1:T(8,128)S(1)}, s32[]{:T(128)}, s32[]{:T(128)}, /*index=5*/s32[]{:T(128)}) while((s32[]{:T(128)}, f32[32,32]{0,1:T(8,128)S(1)}, f32[32,32]{0,1:T(8,128)S(1)}, s32[]{:T(128)}, s32[]{:T(128)}, /*index=5*/s32[]{:T(128)}) %tuple.1853), condition=%wide.region_30.31_spmd.clone.clone, body=%wide.region_29.30_spmd.clone.clone.sunk | while | flops 4292 | bytes 19003 | solution.py:61
  1326.6 43.6 %while.686 = (s32[]{:T(128)}, f32[32,32]{1,0:T(8,128)S(1)}, f32[32,32]{1,0:T(8,128)S(1)}, f32[32,32]{0,1:T(8,128)S(1)}, s32[]{:T(128)}, /*index=5*/s32[]{:T(128)}, s32[]{:T(128)}) while((s32[]{:T(128)}, f32[32,32]{1,0:T(8,128)S(1)}, f32[32,32]{1,0:T(8,128)S(1)}, f32[32,32]{0,1:T(8,128)S(1)}, s32[]{:T(128)}, ...), condition=%wide.region_32.33_spmd.clone.clone, body=%wide.region_31.32_spmd.clone.clone.sunk | while | flops 4228 | bytes 18367 | solution.py:79
  1371.0 45.0 %while.687 = (s32[]{:T(128)}, f32[32,32]{0,1:T(8,128)S(1)}, f32[32,32]{0,1:T(8,128)S(1)}, s32[]{:T(128)}, s32[]{:T(128)}, /*index=5*/s32[]{:T(128)}) while((s32[]{:T(128)}, f32[32,32]{0,1:T(8,128)S(1)}, f32[32,32]{0,1:T(8,128)S(1)}, s32[]{:T(128)}, s32[]{:T(128)}, /*index=5*/s32[]{:T(128)}) %tuple.1789), condition=%wide.region_34.35_spmd.clone.clone, body=%wide.region_33.34_spmd.clone.clone.sunk | while | flops 4292 | bytes 19003 | solution.py:61
  1416.1 43.6 %while.688 = (s32[]{:T(128)}, f32[32,32]{1,0:T(8,128)S(1)}, f32[32,32]{1,0:T(8,128)S(1)}, f32[32,32]{0,1:T(8,128)S(1)}, s32[]{:T(128)}, /*index=5*/s32[]{:T(128)}, s32[]{:T(128)}) while((s32[]{:T(128)}, f32[32,32]{1,0:T(8,128)S(1)}, f32[32,32]{1,0:T(8,128)S(1)}, f32[32,32]{0,1:T(8,128)S(1)}, s32[]{:T(128)}, ...), condition=%wide.region_36.37_spmd.clone.clone, body=%wide.region_35.36_spmd.clone.clone.sunk | while | flops 4228 | bytes 18367 | solution.py:79
  1460.5 45.0 %while.689 = (s32[]{:T(128)}, f32[32,32]{0,1:T(8,128)S(1)}, f32[32,32]{0,1:T(8,128)S(1)}, s32[]{:T(128)}, s32[]{:T(128)}, /*index=5*/s32[]{:T(128)}) while((s32[]{:T(128)}, f32[32,32]{0,1:T(8,128)S(1)}, f32[32,32]{0,1:T(8,128)S(1)}, s32[]{:T(128)}, s32[]{:T(128)}, /*index=5*/s32[]{:T(128)}) %tuple.1795), condition=%wide.region_38.39_spmd.clone.clone, body=%wide.region_37.38_spmd.clone.clone.sunk | while | flops 4292 | bytes 19003 | solution.py:61
  1505.5 43.6 %while.690 = (s32[]{:T(128)}, f32[32,32]{1,0:T(8,128)S(1)}, f32[32,32]{1,0:T(8,128)S(1)}, f32[32,32]{0,1:T(8,128)S(1)}, s32[]{:T(128)}, /*index=5*/s32[]{:T(128)}, s32[]{:T(128)}) while((s32[]{:T(128)}, f32[32,32]{1,0:T(8,128)S(1)}, f32[32,32]{1,0:T(8,128)S(1)}, f32[32,32]{0,1:T(8,128)S(1)}, s32[]{:T(128)}, ...), condition=%wide.region_40.41_spmd.clone.clone, body=%wide.region_39.40_spmd.clone.clone.sunk | while | flops 4228 | bytes 18367 | solution.py:79
  1549.8 45.0 %while.691 = (s32[]{:T(128)}, f32[32,32]{0,1:T(8,128)S(1)}, f32[32,32]{0,1:T(8,128)S(1)}, s32[]{:T(128)}, s32[]{:T(128)}, /*index=5*/s32[]{:T(128)}) while((s32[]{:T(128)}, f32[32,32]{0,1:T(8,128)S(1)}, f32[32,32]{0,1:T(8,128)S(1)}, s32[]{:T(128)}, s32[]{:T(128)}, /*index=5*/s32[]{:T(128)}) %tuple.1801), condition=%wide.region_42.43_spmd.clone.clone, body=%wide.region_41.42_spmd.clone.clone.sunk | while | flops 4292 | bytes 19003 | solution.py:61
  1594.9 43.6 %while.692 = (s32[]{:T(128)}, f32[32,32]{1,0:T(8,128)S(1)}, f32[32,32]{1,0:T(8,128)S(1)}, f32[32,32]{0,1:T(8,128)S(1)}, s32[]{:T(128)}, /*index=5*/s32[]{:T(128)}, s32[]{:T(128)}) while((s32[]{:T(128)}, f32[32,32]{1,0:T(8,128)S(1)}, f32[32,32]{1,0:T(8,128)S(1)}, f32[32,32]{0,1:T(8,128)S(1)}, s32[]{:T(128)}, ...), condition=%wide.region_44.45_spmd.clone.clone, body=%wide.region_43.44_spmd.clone.clone.sunk | while | flops 4228 | bytes 18367 | solution.py:79
  1639.2 45.0 %while.693 = (s32[]{:T(128)}, f32[32,32]{0,1:T(8,128)S(1)}, f32[32,32]{0,1:T(8,128)S(1)}, s32[]{:T(128)}, s32[]{:T(128)}, /*index=5*/s32[]{:T(128)}) while((s32[]{:T(128)}, f32[32,32]{0,1:T(8,128)S(1)}, f32[32,32]{0,1:T(8,128)S(1)}, s32[]{:T(128)}, s32[]{:T(128)}, /*index=5*/s32[]{:T(128)}) %tuple.1807), condition=%wide.region_46.47_spmd.clone.clone, body=%wide.region_45.46_spmd.clone.clone.sunk | while | flops 4292 | bytes 19003 | solution.py:61
  1691.8 43.6 %while.694 = (s32[]{:T(128)}, f32[32,32]{1,0:T(8,128)S(1)}, f32[32,32]{1,0:T(8,128)S(1)}, f32[32,32]{0,1:T(8,128)S(1)}, s32[]{:T(128)}, /*index=5*/s32[]{:T(128)}, s32[]{:T(128)}) while((s32[]{:T(128)}, f32[32,32]{1,0:T(8,128)S(1)}, f32[32,32]{1,0:T(8,128)S(1)}, f32[32,32]{0,1:T(8,128)S(1)}, s32[]{:T(128)}, ...), condition=%wide.region_48.49_spmd.clone.clone, body=%wide.region_47.48_spmd.clone.clone.sunk | while | flops 4228 | bytes 18367 | solution.py:79
  1736.0 45.0 %while.695 = (s32[]{:T(128)}, f32[32,32]{0,1:T(8,128)S(1)}, f32[32,32]{0,1:T(8,128)S(1)}, s32[]{:T(128)}, s32[]{:T(128)}, /*index=5*/s32[]{:T(128)}) while((s32[]{:T(128)}, f32[32,32]{0,1:T(8,128)S(1)}, f32[32,32]{0,1:T(8,128)S(1)}, s32[]{:T(128)}, s32[]{:T(128)}, /*index=5*/s32[]{:T(128)}) %tuple.1813), condition=%wide.region_50.51_spmd.clone.clone, body=%wide.region_49.50_spmd.clone.clone.sunk | while | flops 4292 | bytes 19003 | solution.py:61
  1781.0 43.6 %while.696 = (s32[]{:T(128)}, f32[32,32]{1,0:T(8,128)S(1)}, f32[32,32]{1,0:T(8,128)S(1)}, f32[32,32]{0,1:T(8,128)S(1)}, s32[]{:T(128)}, /*index=5*/s32[]{:T(128)}, s32[]{:T(128)}) while((s32[]{:T(128)}, f32[32,32]{1,0:T(8,128)S(1)}, f32[32,32]{1,0:T(8,128)S(1)}, f32[32,32]{0,1:T(8,128)S(1)}, s32[]{:T(128)}, ...), condition=%wide.region_52.53_spmd.clone.clone, body=%wide.region_51.52_spmd.clone.clone.sunk | while | flops 4228 | bytes 18367 | solution.py:79
  1825.1 45.0 %while.697 = (s32[]{:T(128)}, f32[32,32]{0,1:T(8,128)S(1)}, f32[32,32]{0,1:T(8,128)S(1)}, s32[]{:T(128)}, s32[]{:T(128)}, /*index=5*/s32[]{:T(128)}) while((s32[]{:T(128)}, f32[32,32]{0,1:T(8,128)S(1)}, f32[32,32]{0,1:T(8,128)S(1)}, s32[]{:T(128)}, s32[]{:T(128)}, /*index=5*/s32[]{:T(128)}) %tuple.1819), condition=%wide.region_54.55_spmd.clone.clone, body=%wide.region_53.54_spmd.clone.clone.sunk | while | flops 4292 | bytes 19003 | solution.py:61
  1870.2 43.6 %while.698 = (s32[]{:T(128)}, f32[32,32]{1,0:T(8,128)S(1)}, f32[32,32]{1,0:T(8,128)S(1)}, f32[32,32]{0,1:T(8,128)S(1)}, s32[]{:T(128)}, /*index=5*/s32[]{:T(128)}, s32[]{:T(128)}) while((s32[]{:T(128)}, f32[32,32]{1,0:T(8,128)S(1)}, f32[32,32]{1,0:T(8,128)S(1)}, f32[32,32]{0,1:T(8,128)S(1)}, s32[]{:T(128)}, ...), condition=%wide.region_56.57_spmd.clone.clone, body=%wide.region_55.56_spmd.clone.clone.sunk | while | flops 4228 | bytes 18367 | solution.py:79
  1914.3 45.0 %while.699 = (s32[]{:T(128)}, f32[32,32]{0,1:T(8,128)S(1)}, f32[32,32]{0,1:T(8,128)S(1)}, s32[]{:T(128)}, s32[]{:T(128)}, /*index=5*/s32[]{:T(128)}) while((s32[]{:T(128)}, f32[32,32]{0,1:T(8,128)S(1)}, f32[32,32]{0,1:T(8,128)S(1)}, s32[]{:T(128)}, s32[]{:T(128)}, /*index=5*/s32[]{:T(128)}) %tuple.1825), condition=%wide.region_58.59_spmd.clone.clone, body=%wide.region_57.58_spmd.clone.clone.sunk | while | flops 4292 | bytes 19003 | solution.py:61
  1959.4 43.6 %while.700 = (s32[]{:T(128)}, f32[32,32]{1,0:T(8,128)S(1)}, f32[32,32]{1,0:T(8,128)S(1)}, f32[32,32]{0,1:T(8,128)S(1)}, s32[]{:T(128)}, /*index=5*/s32[]{:T(128)}, s32[]{:T(128)}) while((s32[]{:T(128)}, f32[32,32]{1,0:T(8,128)S(1)}, f32[32,32]{1,0:T(8,128)S(1)}, f32[32,32]{0,1:T(8,128)S(1)}, s32[]{:T(128)}, ...), condition=%wide.region_60.61_spmd.clone.clone, body=%wide.region_59.60_spmd.clone.clone.sunk | while | flops 4228 | bytes 18367 | solution.py:79
  2016.5 45.0 %while.701 = (s32[]{:T(128)}, f32[32,32]{0,1:T(8,128)S(1)}, f32[32,32]{0,1:T(8,128)S(1)}, s32[]{:T(128)}, s32[]{:T(128)}, /*index=5*/s32[]{:T(128)}) while((s32[]{:T(128)}, f32[32,32]{0,1:T(8,128)S(1)}, f32[32,32]{0,1:T(8,128)S(1)}, s32[]{:T(128)}, s32[]{:T(128)}, /*index=5*/s32[]{:T(128)}) %tuple.1857), condition=%wide.region_62.63_spmd.clone.clone, body=%wide.region_61.62_spmd.clone.clone.sunk | while | flops 4292 | bytes 19003 | solution.py:61
  2061.5 43.6 %while.702 = (s32[]{:T(128)}, f32[32,32]{1,0:T(8,128)S(1)}, f32[32,32]{1,0:T(8,128)S(1)}, f32[32,32]{0,1:T(8,128)S(1)}, s32[]{:T(128)}, /*index=5*/s32[]{:T(128)}, s32[]{:T(128)}) while((s32[]{:T(128)}, f32[32,32]{1,0:T(8,128)S(1)}, f32[32,32]{1,0:T(8,128)S(1)}, f32[32,32]{0,1:T(8,128)S(1)}, s32[]{:T(128)}, ...), condition=%wide.region_64.65_spmd.clone.clone, body=%wide.region_63.64_spmd.clone.clone.sunk | while | flops 4228 | bytes 18367 | solution.py:79
  (5422 shorter events, 1197.8 us)
Async XLA Ops:
  7.2 538.7 %all-reduce.4.cloned.1.call-start = ((), (), s32[]{:S(2)}) async-start(), calls=%async_computation.1 | async-start | bytes 4194304 | tf_op jit(solution)/shard_map/psum | solution.py:160
  8.1 5.4 collective-permute-start
  12.1 4.4 collective-permute-start.1
  62.1 1.3 copy-start.15
  66.1 0.7 copy-start.24
  66.1 1.6 copy-start.16
  66.1 573.3 %copy-start = (f32[32,32]{1,0:T(8,128)}, f32[32,32]{1,0:T(8,128)S(1)}, u32[]{:S(2)}) copy-start(f32[32,32]{1,0:T(8,128)S(1)} %fusion.258) | copy-start | bytes 12292
  639.5 135.1 %copy-start.2 = (f32[32,32]{1,0:T(8,128)S(1)}, f32[32,32]{1,0:T(8,128)}, u32[]{:S(2)}) copy-start(f32[32,32]{1,0:T(8,128)} %copy-done) | copy-start | bytes 12292
  728.2 91.3 %copy-start.22 = (f32[32,32]{0,1:T(8,128)}, f32[32,32]{0,1:T(8,128)S(1)}, u32[]{:S(2)}) copy-start(f32[32,32]{0,1:T(8,128)S(1)} %get-tuple-element.7857) | copy-start | bytes 12292
  818.2 1.4 copy-start.21
  818.6 98.3 %copy-start.3 = (f32[32,32]{1,0:T(8,128)S(1)}, f32[32,32]{1,0:T(8,128)}, u32[]{:S(2)}) copy-start(f32[32,32]{1,0:T(8,128)} %copy-done) | copy-start | bytes 12292
  819.6 184.9 %copy-start.20 = (f32[32,32]{0,1:T(8,128)S(1)}, f32[32,32]{0,1:T(8,128)}, u32[]{:S(2)}) copy-start(f32[32,32]{0,1:T(8,128)} %custom-call.8) | copy-start | bytes 12292
  906.2 143.3 %copy-start.4 = (f32[32,32]{1,0:T(8,128)S(1)}, f32[32,32]{1,0:T(8,128)}, u32[]{:S(2)}) copy-start(f32[32,32]{1,0:T(8,128)} %copy-done) | copy-start | bytes 12292
  1003.3 90.8 %copy-start.19 = (f32[32,32]{0,1:T(8,128)S(1)}, f32[32,32]{0,1:T(8,128)}, u32[]{:S(2)}) copy-start(f32[32,32]{0,1:T(8,128)} %custom-call.10) | copy-start | bytes 12292
  1003.7 135.5 %copy-start.5 = (f32[32,32]{1,0:T(8,128)S(1)}, f32[32,32]{1,0:T(8,128)}, u32[]{:S(2)}) copy-start(f32[32,32]{1,0:T(8,128)} %copy-done) | copy-start | bytes 12292
  1093.1 90.7 %copy-start.18 = (f32[32,32]{0,1:T(8,128)S(1)}, f32[32,32]{0,1:T(8,128)}, u32[]{:S(2)}) copy-start(f32[32,32]{0,1:T(8,128)} %custom-call.12) | copy-start | bytes 12292
  1093.4 135.4 %copy-start.6 = (f32[32,32]{1,0:T(8,128)S(1)}, f32[32,32]{1,0:T(8,128)}, u32[]{:S(2)}) copy-start(f32[32,32]{1,0:T(8,128)} %copy-done) | copy-start | bytes 12292
  1139.2 134.2 %copy-start.17 = (f32[32,32]{0,1:T(8,128)S(1)}, f32[32,32]{0,1:T(8,128)}, u32[]{:S(2)}) copy-start(f32[32,32]{0,1:T(8,128)} %custom-call.14) | copy-start | bytes 12292
  1183.0 143.6 %copy-start.7 = (f32[32,32]{1,0:T(8,128)S(1)}, f32[32,32]{1,0:T(8,128)}, u32[]{:S(2)}) copy-start(f32[32,32]{1,0:T(8,128)} %copy-done) | copy-start | bytes 12292
  1272.7 143.4 %copy-start.8 = (f32[32,32]{1,0:T(8,128)S(1)}, f32[32,32]{1,0:T(8,128)}, u32[]{:S(2)}) copy-start(f32[32,32]{1,0:T(8,128)} %copy-done) | copy-start | bytes 12292
  1322.9 182.6 %copy-start.9 = (f32[32,32]{1,0:T(8,128)S(1)}, f32[32,32]{1,0:T(8,128)}, u32[]{:S(2)}) copy-start(f32[32,32]{1,0:T(8,128)} %copy-done) | copy-start | bytes 12292
  1371.0 223.8 %copy-start.10 = (f32[32,32]{1,0:T(8,128)S(1)}, f32[32,32]{1,0:T(8,128)}, u32[]{:S(2)}) copy-start(f32[32,32]{1,0:T(8,128)} %copy-done) | copy-start | bytes 12292
  1505.5 186.3 %copy-start.11 = (f32[32,32]{1,0:T(8,128)S(1)}, f32[32,32]{1,0:T(8,128)}, u32[]{:S(2)}) copy-start(f32[32,32]{1,0:T(8,128)} %copy-done) | copy-start | bytes 12292
  1549.8 231.2 %copy-start.12 = (f32[32,32]{1,0:T(8,128)S(1)}, f32[32,32]{1,0:T(8,128)}, u32[]{:S(2)}) copy-start(f32[32,32]{1,0:T(8,128)} %copy-done) | copy-start | bytes 12292
  1638.7 231.5 %copy-start.13 = (f32[32,32]{1,0:T(8,128)S(1)}, f32[32,32]{1,0:T(8,128)}, u32[]{:S(2)}) copy-start(f32[32,32]{1,0:T(8,128)} %copy-done) | copy-start | bytes 12292
  1691.8 267.6 %copy-start.14 = (f32[32,32]{1,0:T(8,128)S(1)}, f32[32,32]{1,0:T(8,128)}, u32[]{:S(2)}) copy-start(f32[32,32]{1,0:T(8,128)} %copy-done) | copy-start | bytes 12292
  1913.8 102.7 %copy-start.23 = (f32[32,32]{0,1:T(8,128)S(1)}, f32[32,32]{0,1:T(8,128)}, u32[]{:S(2)}) copy-start(f32[32,32]{0,1:T(8,128)} %custom-call.30) | copy-start | bytes 12292
  1959.4 102.1 %copy-start.1 = (f32[32,32]{1,0:T(8,128)S(1)}, f32[32,32]{1,0:T(8,128)}, u32[]{:S(2)}) copy-start(f32[32,32]{1,0:T(8,128)} %copy-done) | copy-start | bytes 12292
  2133.2 0.7 copy-start.25
Sparse Core Ops, SparseCore 0:
  66.2 479.6 all-reduce.3
where the time goes:
time: 2160 us; the launch traced here: 2140 us
  local copies, waits for them, and re-layouts  667 us (31%)
  other arithmetic  500 us (23%)
  loops' own time  382 us (18%)
  waiting for transfers between devices  371 us (17%)
  blocking collectives  144 us (7%)
  matrix products  56.1 us (3%)
    another operation x16, loops' own time, small_factor(): lax.fori_loop(0, order, column_step, (matrix, jnp.zeros_like(matrix)))[1]  369 us
    psum x1, waiting for transfers between devices, shards(): gram_block, projected = lax.psum((gram_block, projected), ('rows', 'cols'))  368 us
    mul x1024, other arithmetic, row_step(): rest = rest - below[:, None] * value  363 us
    dynamic_slice x512, local copies, waits for them, and re-layouts, row_step(): pivot = lax.dynamic_slice_in_dim(column, index_row, 1, 0)[0]  322 us
    dynamic_slice x512, local copies, waits for them, and re-layouts, column_step(): pivot = jnp.sqrt(lax.dynamic_slice_in_dim(column, index_col, 1, 0)[0])  301 us
    psum x1, blocking collectives, shards(): gram_block, projected = lax.psum((gram_block, projected), ('rows', 'cols'))  110 us
    select_n x512, other arithmetic, column_step(): lower = jnp.where(positions[None, :] == index_col, column[:, None], lower)  80.9 us
    dot_general x123, matrix products, matmul(): jnp.dot(left, right, precision=lax.Precision.HIGHEST, preferred_element_t...  46.5 us

commit v1 on v0

v1 whole, which is shorter than its diff:
```python
import functools

import jax
import jax.numpy as jnp
from jax import lax
from jax.experimental import pallas as pl
from jax.experimental.pallas import tpu as pltpu
from jax.sharding import PartitionSpec as P

TILE = 128
BLK = 128
NX = 4
NY = 4
MESH = pl.DeviceIdType.MESH
HIGHEST = lax.Precision.HIGHEST
HEAD = [(a, b) for a in range(4) for b in range(a, 4)]
COUNT = (3, 3, 4, 4)
FIRST = (0, 3, 6, 10)
HALF = 14


def slot_of(core, x, y):
    if x < 2:
        spot = (core * 2 + x) * 3 + y
        if spot < len(HEAD):
            return HEAD[spot]
        return "proj" if spot == len(HEAD) else None
    return (y, x * 2 + core)


def gram_kernel(
    n_rows,
    base_ref, field_ref, grad_ref, tile_ref, type_ref,
    head_ref, own_ref,
    raw, jac, codes_mine, codes, north, south, parts,
    from_core, half, from_x, quarter, from_y, block, from_z, piece,
    line, panel, head_half,
    a2a_send, a2a_recv, code_send, code_recv, halo_send, halo_recv,
    core_sems, x_send, x_recv, y_send, y_recv, z_send, z_recv,
    zg_send, zg_recv, yg_send, yg_recv, xg_send, xg_recv, cg_send, cg_recv,
):
    r = lax.axis_index("rows")
    c = lax.axis_index("cols")
    nz = n_rows // NY
    z, y = r // NY, r % NY
    x, core = c // 2, c % 2
    up, down = (r + n_rows - 1) % n_rows, (r + 1) % n_rows
    cells = raw.shape[1]

    def dev_c(col):
        return (r, col)

    def dev_y(yy):
        return (z * NY + yy, c)

    def dev_z(zz):
        return (zz * NY + y, c)

    def remote(src, dst, send, recv, device):
        return pltpu.make_async_remote_copy(
            src_ref=src, dst_ref=dst, send_sem=send, recv_sem=recv,
            device_id=device, device_id_type=MESH,
        )

    barrier = pltpu.get_barrier_semaphore()

    def greet(device):
        pl.semaphore_signal(barrier, inc=1, device_id=device, device_id_type=MESH)

    for d in range(1, 8):
        greet(dev_c((c + d) % 8))
    for d in range(1, NY):
        greet(dev_y((y + d) % NY))
    for d in range(1, nz):
        greet(dev_z((z + d) % nz))
    greet((up, c))
    greet((down, c))
    codes_mine[...] = jnp.zeros_like(codes_mine)
    codes_mine[0:1, :] = tile_ref[...]
    codes_mine[1:2, :] = type_ref[...]
    pl.semaphore_wait(barrier, 7 + (NY - 1) + (nz - 1) + 2)

    sent = []
    for d in range(1, 8):
        to = (c + d) % 8
        cp = remote(codes_mine, codes.at[c], code_send.at[d], code_recv.at[d], dev_c(to))
        cp.start()
        sent.append(cp)
    cp = remote(field_ref, north, halo_send.at[0], halo_recv.at[0], (down, c))
    cp.start()
    sent.append(cp)
    cp = remote(field_ref, south, halo_send.at[1], halo_recv.at[1], (up, c))
    cp.start()
    sent.append(cp)
    for d in (4, 3, 5, 2, 6, 1, 7):
        to = (c + d) % 8
        cp = remote(
            base_ref.at[pl.ds(to * cells, cells), :], raw.at[c],
            a2a_send.at[d], a2a_recv.at[d], dev_c(to),
        )
        cp.start()
        sent.append(cp)
    mine = pltpu.make_async_copy(
        base_ref.at[pl.ds(c * cells, cells), :], raw.at[c], a2a_recv.at[0]
    )
    mine.start()
    codes[c] = codes_mine[...]

    remote(field_ref, north, halo_send.at[0], halo_recv.at[0], (up, c)).wait_recv()
    remote(field_ref, south, halo_send.at[1], halo_recv.at[1], (down, c)).wait_recv()
    here = field_ref[pl.ds(c, 1), :]
    above = field_ref[pl.ds((c + 7) % 8, 1), :]
    below = field_ref[pl.ds((c + 1) % 8, 1), :]
    above = jnp.where(c == 0, jnp.where(r == 0, 0.0, north[7:8, :]), above)
    below = jnp.where(c == 7, jnp.where(r == n_rows - 1, 0.0, south[0:1, :]), below)
    wide = (8, cells)
    here = jnp.broadcast_to(here, wide)
    above = jnp.broadcast_to(above, wide)
    below = jnp.broadcast_to(below, wide)
    lane = lax.broadcasted_iota(jnp.int32, wide, 1)
    west = jnp.where(lane == 0, 0.0, pltpu.roll(here, 1, 1))
    east = jnp.where(lane == cells - 1, 0.0, pltpu.roll(here, cells - 1, 1))
    laplace = 4.0 * here - (above + below + west + east)
    slope_x = 0.5 * (east - west)
    slope_y = 0.5 * (below - above)
    srow = lax.broadcasted_iota(jnp.int32, wide, 0)
    terms = []
    for fieldval in (laplace, slope_x, slope_y):
        rest = fieldval / TILE
        for _ in range(3):
            term = rest.astype(jnp.bfloat16).astype(jnp.float32)
            terms.append(term)
            rest = rest - term
    low = jnp.zeros(wide, jnp.float32)
    for k in range(8):
        low = jnp.where(srow == k, terms[(k % 3) * 3 + k // 3], low)
    high = jnp.where(srow == 0, terms[2 * 3 + 2], 0.0)
    both = jnp.concatenate([low, high], axis=0)
    tiles = cells // TILE
    spread = jnp.concatenate([both] * tiles, axis=0)
    krow = lax.broadcasted_iota(jnp.int32, spread.shape, 0)
    kcol = lax.broadcasted_iota(jnp.int32, spread.shape, 1)
    spread = jnp.where(krow // 16 == kcol // TILE, spread, 0.0)
    spread_t = spread.T.astype(jnp.bfloat16)

    first_tile = (r * 8 // TILE) * tiles
    rows16 = lax.broadcasted_iota(jnp.int32, (16 * tiles, BLK), 0)
    term_id = rows16 % 16
    kind_of = jnp.where(term_id < 9, term_id % 3, 3)
    tile_of = first_tile + rows16 // 16
    for d in range(1, 8):
        src = (c + 8 - d) % 8
        remote(codes_mine, codes.at[src], code_send.at[d], code_recv.at[d], dev_c(src)).wait_recv()

    for cs in range(8):
        @pl.when(c == cs)
        def _():
            mine.wait()

        @pl.when(c != cs)
        def _():
            d = (c + 8 - cs) % 8
            remote(
                base_ref.at[pl.ds(0, cells), :], raw.at[cs],
                a2a_send.at[d], a2a_recv.at[d], dev_c(cs),
            ).wait_recv()

        chosen = jnp.logical_and(
            kind_of == codes[cs, 1:2, :], tile_of == codes[cs, 0:1, :]
        ).astype(jnp.float32).astype(jnp.bfloat16)
        added = jnp.dot(spread_t, chosen, preferred_element_type=jnp.float32)
        jac[:, cs * BLK:(cs + 1) * BLK] = (raw[cs].astype(jnp.float32) + added).astype(jnp.bfloat16)

    where = {slot_of(k, xx, yy): k * HALF + FIRST[xx] + yy
             for k in range(2) for xx in range(NX) for yy in range(COUNT[xx])}
    contract = (((0,), (0,)), ((), ()))
    for pa in range(2):
        left = jac[:, pa * 256:(pa + 1) * 256]
        for pb in range(pa, 4):
            prod = lax.dot_general(
                left, jac[:, pb * 256:(pb + 1) * 256], contract,
                preferred_element_type=jnp.float32,
            )
            for i in range(2):
                for j in range(2):
                    key = (pa * 2 + i, pb * 2 + j)
                    if key in where:
                        parts[where[key]] = prod[i * BLK:(i + 1) * BLK, j * BLK:(j + 1) * BLK]
    proj = jnp.dot(grad_ref[...], jac[:, 0:512], preferred_element_type=jnp.float32)
    proj = jnp.sum(
        jnp.where(lax.broadcasted_iota(jnp.int32, proj.shape, 0) == c, proj, 0.0),
        axis=0, keepdims=True,
    )
    parts[where["proj"]] = jnp.zeros((BLK, BLK), jnp.float32)
    parts[where[None]] = jnp.zeros((BLK, BLK), jnp.float32)
    for k in range(4):
        parts[where["proj"], k:k + 1, :] = proj[:, k * BLK:(k + 1) * BLK]

    cp = remote(
        parts.at[pl.ds((1 - core) * HALF, HALF)], from_core,
        core_sems.at[0], core_sems.at[1], dev_c(x * 2 + 1 - core),
    )
    cp.start()
    sent.append(cp)
    cp.wait_recv()
    half[...] = parts[pl.ds(core * HALF, HALF)] + from_core[...]

    for xx in range(NX):
        span = COUNT[xx]

        @pl.when(x != xx)
        def _():
            d = (xx + NX - x) % NX
            remote(
                half.at[pl.ds(FIRST[xx], span)], from_x.at[d, pl.ds(0, span)],
                x_send.at[d], x_recv.at[d], dev_c(xx * 2 + core),
            ).start()

    for xx in range(NX):
        span = COUNT[xx]

        @pl.when(x == xx)
        def _():
            total = half[FIRST[xx]:FIRST[xx] + span]
            for d in (1, 3, 2):
                remote(
                    half.at[pl.ds(FIRST[xx], span)], from_x.at[d, pl.ds(0, span)],
                    x_send.at[d], x_recv.at[d], dev_c(((xx + NX - d) % NX) * 2 + core),
                ).wait_recv()
                total = total + from_x[d, 0:span]
            quarter[0:span] = total

    holds = jnp.logical_or(x >= 2, y < 3)

    def y_copy(d, yy, peer):
        return remote(
            quarter.at[yy], from_y.at[d], y_send.at[d], y_recv.at[d], dev_y(peer)
        )

    for d in range(1, NY):
        yy = (y + d) % NY

        @pl.when(jnp.logical_or(x >= 2, yy < 3))
        def _():
            y_copy(d, yy, yy).start()

    def z_copy(d, zz, peer):
        return remote(
            block.at[pl.ds(zz * 8, 8)], from_z.at[d], z_send.at[d], z_recv.at[d], dev_z(peer)
        )

    def zg_copy(d, spot, peer):
        return remote(
            piece, line.at[pl.ds(spot * 8, 8)], zg_send.at[d], zg_recv.at[d], dev_z(peer)
        )

    def yg_copy(d, spot, peer):
        return remote(
            line, panel.at[spot], yg_send.at[d], yg_recv.at[d], dev_y(peer)
        )

    @pl.when(holds)
    def _():
        total = quarter[y]
        for d in range(1, NY):
            y_copy(d, 0, (y + NY - d) % NY).wait_recv()
            total = total + from_y[d]
        block[...] = total
        for d in range(1, nz):
            zz = (z + d) % nz
            z_copy(d, zz, zz).start()
        total = block[pl.ds(pl.multiple_of(z * 8, 8), 8)]
        for d in range(1, nz):
            z_copy(d, 0, (z + nz - d) % nz).wait_recv()
            total = total + from_z[d]
        piece[...] = total
        for d in range(1, nz):
            zg_copy(d, z, (z + d) % nz).start()
        line[pl.ds(pl.multiple_of(z * 8, 8), 8)] = total
        for d in range(1, nz):
            src = (z + nz - d) % nz
            zg_copy(d, src, src).wait_recv()
        for d in range(1, NY):
            yg_copy(d, y, (y + d) % NY).start()
        panel[y] = line[...]

    for d in range(1, NY):
        src = (y + NY - d) % NY

        @pl.when(jnp.logical_or(x >= 2, src < 3))
        def _():
            yg_copy(d, src, src).wait_recv()

    def xg_copy(d, xx, peer):
        return remote(
            panel.at[pl.ds(0, 3)], head_half.at[xx], xg_send.at[d], xg_recv.at[d],
            dev_c(peer * 2 + core),
        )

    def cg_copy(xx):
        return remote(
            head_half.at[xx], head_ref.at[pl.ds((core * 2 + xx) * 3, 3)],
            cg_send.at[xx], cg_recv.at[xx], dev_c(x * 2 + 1 - core),
        )

    @pl.when(x < 2)
    def _():
        for d in range(1, NX):
            xg_copy(d, x, (x + d) % NX).start()
        head_half[x] = panel[0:3]

    for xx in range(2):
        @pl.when(x != xx)
        def _():
            d = (x + NX - xx) % NX
            xg_copy(d, xx, xx).wait_recv()

        cg_copy(xx).start()
        head_ref[pl.ds((core * 2 + xx) * 3, 3)] = head_half[xx]

    @pl.when(x >= 2)
    def _():
        own_ref[...] = panel[...]

    @pl.when(x < 2)
    def _():
        own_ref[...] = jnp.zeros_like(own_ref)

    for xx in range(2):
        remote(
            head_half.at[xx], head_ref.at[pl.ds(((1 - core) * 2 + xx) * 3, 3)],
            cg_send.at[xx], cg_recv.at[xx], dev_c(x * 2 + 1 - core),
        ).wait_recv()

    for cp in sent:
        cp.wait_send()
    for xx in range(NX):
        @pl.when(x != xx)
        def _():
            d = (xx + NX - x) % NX
            remote(
                half.at[pl.ds(FIRST[xx], COUNT[xx])], from_x.at[d, pl.ds(0, COUNT[xx])],
                x_send.at[d], x_recv.at[d], dev_c(xx * 2 + core),
            ).wait_send()
    for d in range(1, NY):
        yy = (y + d) % NY

        @pl.when(jnp.logical_or(x >= 2, yy < 3))
        def _():
            y_copy(d, yy, yy).wait_send()

    @pl.when(holds)
    def _():
        for d in range(1, nz):
            zz = (z + d) % nz
            z_copy(d, zz, zz).wait_send()
            zg_copy(d, z, zz).wait_send()
        for d in range(1, NY):
            yg_copy(d, y, (y + d) % NY).wait_send()

    @pl.when(x < 2)
    def _():
        for d in range(1, NX):
            xg_copy(d, x, (x + d) % NX).wait_send()
    for xx in range(2):
        cg_copy(xx).wait_send()


def gram_everywhere(n_rows, base, field, grad, tile, kind):
    cells = field.shape[1]
    nz = n_rows // NY
    f32 = jnp.float32
    vmem = pl.BlockSpec(memory_space=pltpu.VMEM)
    dma = pltpu.SemaphoreType.DMA
    blocks = lambda *lead: pltpu.VMEM(lead + (BLK, BLK), f32)
    return pl.pallas_call(
        functools.partial(gram_kernel, n_rows),
        out_shape=(
            jax.ShapeDtypeStruct((12, BLK, BLK), f32),
            jax.ShapeDtypeStruct((4, BLK, BLK), f32),
        ),
        in_specs=[pl.BlockSpec(memory_space=pl.ANY), vmem, vmem, vmem, vmem],
        out_specs=(vmem, vmem),
        scratch_shapes=[
            pltpu.VMEM((8, cells, BLK), jnp.bfloat16),
            pltpu.VMEM((cells, 8 * BLK), jnp.bfloat16),
            pltpu.VMEM((8, BLK), jnp.int32),
            pltpu.VMEM((8, 8, BLK), jnp.int32),
            pltpu.VMEM((8, cells), f32),
            pltpu.VMEM((8, cells), f32),
            blocks(2 * HALF), blocks(HALF), blocks(HALF), blocks(NX, 4), blocks(4),
            blocks(NY), blocks(), pltpu.VMEM((nz, 8, BLK), f32), pltpu.VMEM((8, BLK), f32),
            blocks(), blocks(4), blocks(2, 3),
            dma((8,)), dma((8,)), dma((8,)), dma((8,)), dma((2,)), dma((2,)),
            dma((2,)), dma((NX,)), dma((NX,)), dma((NY,)), dma((NY,)), dma((nz,)), dma((nz,)),
            dma((nz,)), dma((nz,)), dma((NY,)), dma((NY,)), dma((NX,)), dma((NX,)),
            dma((2,)), dma((2,)),
        ],
        compiler_params=pltpu.CompilerParams(
            collective_id=0, has_side_effects=True, vmem_limit_bytes=48 << 20
        ),
        name="gram",
    )(base, field, grad, tile, kind)


def dot_f32(left, right, dims=((1,), (0,))):
    return lax.dot_general(
        left, right, (dims, ((), ())), precision=HIGHEST, preferred_element_type=jnp.float32
    )


def across(vec, col):
    return jnp.broadcast_to(vec[:, col:col + 1], (8, BLK))


def along(vec, row):
    return jnp.broadcast_to(vec[row:row + 1, :], (8, BLK))


def eliminate_8(rows8, start):
    cols = [across(rows8, start + t) for t in range(8)]
    entry = [[along(cols[t], s) if t <= s else None for t in range(8)] for s in range(8)]
    inverse = [[None] * 8 for _ in range(8)]
    recip = []
    for t in range(8):
        recip.append(1.0 / entry[t][t])
        for s in range(t + 1, 8):
            factor = entry[s][t] * recip[t]
            for u in range(t + 1, s + 1):
                entry[s][u] = entry[s][u] - factor * entry[u][t]
            for u in range(t):
                inverse[s][u] = inverse[s][u] - factor * inverse[t][u]
            inverse[s][t] = -factor
    return inverse, recip


def factor_block(work, scaled):
    rows = lax.broadcasted_iota(jnp.int32, (8, BLK), 0)
    for q in range(4):
        at = [32 * q + 8 * s for s in range(4)]
        xa = [work[a:a + 8, 0:BLK] for a in at]
        xe = [work[a:a + 8, BLK:2 * BLK] for a in at]
        for s in range(4):
            inverse, recip = eliminate_8(xa[s], at[s])
            new_a, new_e = xa[s], xe[s]
            for t in range(7):
                col = jnp.zeros((8, BLK), jnp.float32)
                for u in range(t + 1, 8):
                    col = jnp.where(rows == u, inverse[u][t], col)
                new_a = new_a + col * along(xa[s], t)
                new_e = new_e + col * along(xe[s], t)
            scale = recip[0]
            for u in range(1, 8):
                scale = jnp.where(rows == u, recip[u], scale)
            scale = jnp.sqrt(scale)
            scaled[at[s]:at[s] + 8, 0:BLK] = new_a * scale
            scaled[at[s]:at[s] + 8, BLK:2 * BLK] = new_e * scale
            row_a = [along(new_a, t) for t in range(8)] if s < 3 else None
            row_e = [along(new_e, t) for t in range(8)] if s < 3 else None
            for later in range(s + 1, 4):
                cols = [across(xa[later], at[s] + u) for u in range(8)]
                for t in range(8):
                    mult = cols[t]
                    for u in range(t):
                        mult = mult + cols[u] * inverse[t][u]
                    mult = mult * recip[t]
                    xa[later] = xa[later] - mult * row_a[t]
                    xe[later] = xe[later] - mult * row_e[t]
        if q < 3:
            low = 32 * (q + 1)
            done = scaled[32 * q:low, :]
            work[low:BLK, :] = work[low:BLK, :] - dot_f32(done[:, low:BLK], done, ((0,), (0,)))


def factor_kernel(head_ref, own_ref, r_ref, m_ref, mat, work, scaled, inv):
    c = lax.axis_index("cols")
    eye = (
        lax.broadcasted_iota(jnp.int32, (BLK, BLK), 0)
        == lax.broadcasted_iota(jnp.int32, (BLK, BLK), 1)
    ).astype(jnp.float32)
    near = jnp.minimum(c, 3)
    for k in range(4):
        for j in range(k, 4):
            mat[k, :, j * BLK:(j + 1) * BLK] = head_ref[HEAD.index((k, j))]
        low, high = jnp.minimum(near, k), jnp.maximum(near, k)
        found = head_ref[low * 4 - low * (low - 1) // 2 + high - low]
        found = jnp.where(k <= near, found, found.T)
        mat[k, :, 512:640] = jnp.where(c >= 4, own_ref[k], found)
        mat[k, :, 640:768] = jnp.broadcast_to(head_ref[len(HEAD), k:k + 1, :], (BLK, BLK)).T
    for k in range(4):
        work[:, 0:BLK] = mat[k, :, k * BLK:(k + 1) * BLK]
        work[:, BLK:2 * BLK] = eye
        factor_block(work, scaled)
        low = (k + 1) * BLK
        inv[k] = scaled[:, BLK:2 * BLK]
        mat[k, :, low:768] = dot_f32(scaled[:, BLK:2 * BLK], mat[k, :, low:768])
        r_ref[k * BLK:(k + 1) * BLK, :] = mat[k, :, 512:640]
        for i in range(k + 1, 4):
            mat[i, :, i * BLK:768] = mat[i, :, i * BLK:768] - dot_f32(
                mat[k, :, i * BLK:(i + 1) * BLK], mat[k, :, i * BLK:768], ((0,), (0,))
            )
    solved = [None] * 4
    for k in (3, 2, 1, 0):
        rest = mat[k, :, 640:768]
        for i in range(k + 1, 4):
            rest = rest - dot_f32(mat[k, :, i * BLK:(i + 1) * BLK], solved[i])
        solved[k] = dot_f32(inv[k], rest, ((0,), (0,)))
        m_ref[k:k + 1, :] = solved[k].T[0:1, :]


def factor_and_solve(head, own):
    f32 = jnp.float32
    vmem = pl.BlockSpec(memory_space=pltpu.VMEM)
    return pl.pallas_call(
        factor_kernel,
        out_shape=(
            jax.ShapeDtypeStruct((512, BLK), f32),
            jax.ShapeDtypeStruct((4, BLK), f32),
        ),
        in_specs=[vmem, vmem],
        out_specs=(vmem, vmem),
        scratch_shapes=[
            pltpu.VMEM((4, BLK, 768), f32),
            pltpu.VMEM((BLK, 2 * BLK), f32),
            pltpu.VMEM((BLK, 2 * BLK), f32),
            pltpu.VMEM((4, BLK, BLK), f32),
        ],
        compiler_params=pltpu.CompilerParams(vmem_limit_bytes=48 << 20),
        name="factor",
    )(head, own)


def shards(n_rows, sens_base, design_field, gradient, tile_index, type_codes):
    head, own = gram_everywhere(
        n_rows, sens_base, design_field, gradient,
        tile_index.reshape(1, BLK), type_codes.reshape(1, BLK),
    )
    r_panels, multipliers = factor_and_solve(head, own)
    return r_panels, multipliers.reshape(-1)


def solution(mesh):
    placed = (P("rows", "cols"), P("rows", None), P("rows", None), P("cols"), P("cols"))
    return jax.shard_map(
        functools.partial(shards, mesh.shape["rows"]),
        mesh=mesh, in_specs=placed, out_specs=(P(None, "cols"), P()), check_vma=False,
    )
```

time: 2160 us -> 123 us (0.06)
  local copies, waits for them, and re-layouts: 667 us -> 4.37 us
  other arithmetic: 500 us -> 0 us
  loops' own time: 382 us -> 0 us
  waiting for transfers between devices: 371 us -> 0 us
  blocking collectives: 144 us -> 0 us
  Pallas kernels: 0 us -> 117 us
  matrix products: 56.1 us -> 0 us
    dynamic_slice x1026 -> x0, local copies, waits for them, and re-layouts: 623 us -> none  [the longest x512 322 us: row_step(): pivot = lax.dynamic_slice_in_dim(column, index_row, 1, 0)[0]]
    another operation x32 -> x0, loops' own time: 382 us -> none  [the longest x16 369 us: small_factor(): lax.fori_loop(0, order, column_step, (matrix, jnp.zeros_like(matrix)))[1]]
    mul x1537 -> x0, other arithmetic: 370 us -> none  [the longest x1024 363 us: row_step(): rest = rest - below[:, None] * value]
    psum x1 -> x0, waiting for transfers between devices: 368 us -> none  [shards(): gram_block, projected = lax.psum((gram_block, projected), ('rows', 'cols'))]
    select_n x1537 -> x0, other arithmetic: 122 us -> none  [the longest x512 80.9 us: column_step(): lower = jnp.where(positions[None, :] == index_col, column[:, None], lower)]
    pallas_call x0 -> x2, Pallas kernels: none -> 117 us  [the longest x1 93.8 us: gram_everywhere(): pl.pallas_call(functools.partial(gram_kernel, n_rows), out_shape=(jax.Sha...]
    psum x1 -> x0, blocking collectives: 110 us -> none  [shards(): gram_block, projected = lax.psum((gram_block, projected), ('rows', 'cols'))]
    dot_general x126 -> x0, matrix products: 56.1 us -> none  [the longest x123 46.5 us: matmul(): jnp.dot(left, right, precision=lax.Precision.HIGHEST, preferred_element_t...]
where the time goes in v1:
time: 123 us; the launch traced here: 122 us
  Pallas kernels  117 us (95%)
  local copies, waits for them, and re-layouts  4.37 us (4%)
    pallas_call x1, Pallas kernels, gram_everywhere(): pl.pallas_call(functools.partial(gram_kernel, n_rows), out_shape=(jax.Sha...  93.8 us
    pallas_call x1, Pallas kernels, factor_and_solve(): pl.pallas_call(factor_kernel, out_shape=(jax.ShapeDtypeStruct((512, BLK),...  23.4 us
    unnamed x10, local copies, waits for them, and re-layouts  4.37 us

profile of v1, /device:TPU:1, one launch (start us, length us, event | category | flops | bytes accessed | tf_op | source)
XLA Modules:
  0.0 122.3 jit_solution(10476388667372307789)
XLA Ops:
  0.6 0.0 copy-start
  0.6 1.6 %copy-done = bf16[8192,128]{1,0:T(8,128)(2,1)S(1)} copy-done((bf16[8192,128]{1,0:T(8,128)(2,1)S(1)}, bf16[8192,128]{1,0:T(8,128)(2,1)}, u32[]{:S(2)}) %copy-start) | copy-done | bytes 2097176
  2.2 0.0 copy-start.1
  2.2 0.8 copy-done.1
  3.0 0.0 copy-start.2
  3.0 0.7 copy-done.2
  3.7 0.0 copy-start.3
  3.7 0.7 copy-done.3
  4.4 0.0 copy-start.4
  4.4 0.7 copy-done.4
  5.0 93.8 %gram.1 = (f32[12,128,128]{2,1,0:T(8,128)S(1)}, f32[4,128,128]{2,1,0:T(8,128)S(1)}) custom-call(bf16[8192,128]{1,0:T(8,128)(2,1)S(1)} %copy-done, f32[8,1024]{1,0:T(8,128)S(1)} %copy-done.1, bf16[8,1024]{1,0:T(8,128)(2,1)S(1)} %copy-done.2, s32[1,128]{1,0:T(1,128)S(1)} %bitcast.3, s32[1,128]{1,0:T(1,128)S(1)} %bitcast.4), custom_call_target="tpu_custom_call" | custom-call | tf_op jit(solution)/shard_map/gram/pallas_call | solution.py:376
  98.8 23.4 %factor.1 = (f32[512,128]{1,0:T(8,128)}, f32[4,128]{1,0:T(4,128)}) custom-call(f32[12,128,128]{2,1,0:T(8,128)S(1)} %get-tuple-element.6.head_ref, f32[4,128,128]{2,1,0:T(8,128)S(1)} %get-tuple-element.7.own_ref), custom_call_target="tpu_custom_call" | custom-call | tf_op jit(solution)/shard_map/factor/pallas_call | solution.py:514
Async XLA Ops:
  0.6 1.6 %copy-start = (bf16[8192,128]{1,0:T(8,128)(2,1)S(1)}, bf16[8192,128]{1,0:T(8,128)(2,1)}, u32[]{:S(2)}) copy-start(bf16[8192,128]{1,0:T(8,128)(2,1)} %base_ref.1) | copy-start | bytes 6291460
  2.2 0.8 copy-start.1
  3.0 0.7 copy-start.2
  3.7 0.7 copy-start.3
  4.4 0.7 copy-start.4

commit v2 on v1

--- a/solution.py
+++ b/solution.py
@@ -14,9 +14,12 @@
 MESH = pl.DeviceIdType.MESH
 HIGHEST = lax.Precision.HIGHEST
 HEAD = [(a, b) for a in range(4) for b in range(a, 4)]
-COUNT = (3, 3, 4, 4)
-FIRST = (0, 3, 6, 10)
+COUNT_X = (3, 3, 4, 4)
+FIRST_X = (0, 3, 6, 10)
+COUNT_Y = (4, 4, 4, 2)
+FIRST_Y = (0, 4, 8, 12)
 HALF = 14
+ROWS = BLK // 2
 
 
 def slot_of(core, x, y):
@@ -30,19 +33,22 @@
 
 def gram_kernel(
     n_rows,
-    base_ref, field_ref, grad_ref, tile_ref, type_ref,
-    head_ref, own_ref,
-    raw, jac, codes_mine, codes, north, south, parts,
-    from_core, half, from_x, quarter, from_y, block, from_z, piece,
-    line, panel, head_half,
-    a2a_send, a2a_recv, code_send, code_recv, halo_send, halo_recv,
-    core_sems, x_send, x_recv, y_send, y_recv, z_send, z_recv,
-    zg_send, zg_recv, yg_send, yg_recv, xg_send, xg_recv, cg_send, cg_recv,
+    base_ref, field_hbm, grad_hbm, tile_hbm, type_hbm,
+    out_a, out_b, own_ref,
+    raw, jac, field_ref, grad_ref, tile_ref, type_ref, codes_mine, codes, north, south,
+    parts, from_core, half, from_x, from_y, sum_a, sum_b, from_x2, from_y2,
+    block, from_zl, from_zh, line,
+    load_sems, a2a_send, a2a_recv, code_send, code_recv, halo_send, halo_recv, core_sems,
+    xa_send, xa_recv, yb_send, yb_recv, ya_send, ya_recv, xb_send, xb_recv,
+    zl_send, zl_recv, zh_send, zh_recv, zg_send, zg_recv,
+    gy_send, gy_recv, gx_send, gx_recv, hx_send, hx_recv, hy_send, hy_recv,
+    cg_send, cg_recv,
 ):
     r = lax.axis_index("rows")
     c = lax.axis_index("cols")
-    nz = n_rows // NY
     z, y = r // NY, r % NY
+    zh, zl = z // 4, z % 4
+    hops = n_rows // NY // 4
     x, core = c // 2, c % 2
     up, down = (r + n_rows - 1) % n_rows, (r + 1) % n_rows
     cells = raw.shape[1]
@@ -50,11 +56,14 @@
     def dev_c(col):
         return (r, col)
 
+    def dev_x(xx):
+        return (r, xx * 2 + core)
+
     def dev_y(yy):
         return (z * NY + yy, c)
 
-    def dev_z(zz):
-        return (zz * NY + y, c)
+    def dev_z(hi, lo):
+        return ((hi * 4 + lo) * NY + y, c)
 
     def remote(src, dst, send, recv, device):
         return pltpu.make_async_remote_copy(
@@ -71,14 +80,25 @@
         greet(dev_c((c + d) % 8))
     for d in range(1, NY):
         greet(dev_y((y + d) % NY))
-    for d in range(1, nz):
-        greet(dev_z((z + d) % nz))
+    for d in range(1, 4):
+        greet(dev_z(zh, (zl + d) % 4))
+    for d in range(1, hops):
+        greet(dev_z((zh + d) % hops, zl))
     greet((up, c))
     greet((down, c))
+    loads = []
+    for i, (src, dst) in enumerate((
+        (field_hbm, field_ref), (tile_hbm, tile_ref), (type_hbm, type_ref), (grad_hbm, grad_ref),
+    )):
+        loads.append(pltpu.make_async_copy(src, dst, load_sems.at[i]))
+        loads[-1].start()
     codes_mine[...] = jnp.zeros_like(codes_mine)
+    loads[1].wait()
+    loads[2].wait()
     codes_mine[0:1, :] = tile_ref[...]
     codes_mine[1:2, :] = type_ref[...]
-    pl.semaphore_wait(barrier, 7 + (NY - 1) + (nz - 1) + 2)
+    loads[0].wait()
+    pl.semaphore_wait(barrier, 7 + (NY - 1) + 3 + (hops - 1) + 2)
 
     sent = []
     for d in range(1, 8):
@@ -171,8 +191,18 @@
         added = jnp.dot(spread_t, chosen, preferred_element_type=jnp.float32)
         jac[:, cs * BLK:(cs + 1) * BLK] = (raw[cs].astype(jnp.float32) + added).astype(jnp.bfloat16)
 
-    where = {slot_of(k, xx, yy): k * HALF + FIRST[xx] + yy
-             for k in range(2) for xx in range(NX) for yy in range(COUNT[xx])}
+    where = {}
+    for k in range(2):
+        for xx in range(NX):
+            for yy in range(COUNT_X[xx]):
+                low = FIRST_Y[yy] + (xx if yy < 3 else xx - 2)
+                where[slot_of(k, xx, yy)] = (k, FIRST_X[xx] + yy, HALF + low)
+
+    def put(key, value):
+        k, upper, lower = where[key]
+        parts[k, upper] = value[0:ROWS]
+        parts[k, lower] = value[ROWS:BLK]
+
     contract = (((0,), (0,)), ((), ()))
     for pa in range(2):
         left = jac[:, pa * 256:(pa + 1) * 256]
@@ -185,222 +215,343 @@
                 for j in range(2):
                     key = (pa * 2 + i, pb * 2 + j)
                     if key in where:
-                        parts[where[key]] = prod[i * BLK:(i + 1) * BLK, j * BLK:(j + 1) * BLK]
+                        put(key, prod[i * BLK:(i + 1) * BLK, j * BLK:(j + 1) * BLK])
+    loads[3].wait()
     proj = jnp.dot(grad_ref[...], jac[:, 0:512], preferred_element_type=jnp.float32)
     proj = jnp.sum(
         jnp.where(lax.broadcasted_iota(jnp.int32, proj.shape, 0) == c, proj, 0.0),
         axis=0, keepdims=True,
     )
-    parts[where["proj"]] = jnp.zeros((BLK, BLK), jnp.float32)
-    parts[where[None]] = jnp.zeros((BLK, BLK), jnp.float32)
-    for k in range(4):
-        parts[where["proj"], k:k + 1, :] = proj[:, k * BLK:(k + 1) * BLK]
+    put("proj", jnp.zeros((BLK, BLK), jnp.float32))
+    put(None, jnp.zeros((BLK, BLK), jnp.float32))
+    k, upper, _ = where["proj"]
+    for i in range(4):
+        parts[k, upper, i:i + 1, :] = proj[:, i * BLK:(i + 1) * BLK]
 
     cp = remote(
-        parts.at[pl.ds((1 - core) * HALF, HALF)], from_core,
-        core_sems.at[0], core_sems.at[1], dev_c(x * 2 + 1 - core),
+        parts.at[1 - core], from_core, core_sems.at[0], core_sems.at[1], dev_c(x * 2 + 1 - core)
     )
     cp.start()
     sent.append(cp)
     cp.wait_recv()
-    half[...] = parts[pl.ds(core * HALF, HALF)] + from_core[...]
-
-    for xx in range(NX):
-        span = COUNT[xx]
-
-        @pl.when(x != xx)
-        def _():
-            d = (xx + NX - x) % NX
-            remote(
-                half.at[pl.ds(FIRST[xx], span)], from_x.at[d, pl.ds(0, span)],
-                x_send.at[d], x_recv.at[d], dev_c(xx * 2 + core),
-            ).start()
-
-    for xx in range(NX):
-        span = COUNT[xx]
-
-        @pl.when(x == xx)
-        def _():
-            total = half[FIRST[xx]:FIRST[xx] + span]
+    half[...] = parts[core] + from_core[...]
+
+    def xa_copy(xx, d, peer):
+        span = COUNT_X[xx]
+        return remote(
+            half.at[pl.ds(FIRST_X[xx], span)], from_x.at[d, pl.ds(0, span)],
+            xa_send.at[d], xa_recv.at[d], dev_x(peer),
+        )
+
+    def yb_copy(yy, d, peer):
+        span = COUNT_Y[yy]
+        return remote(
+            half.at[pl.ds(HALF + FIRST_Y[yy], span)], from_y.at[d, pl.ds(0, span)],
+            yb_send.at[d], yb_recv.at[d], dev_y(peer),
+        )
+
+    for q in range(4):
+        @pl.when(x != q)
+        def _():
+            xa_copy(q, (q + NX - x) % NX, q).start()
+
+        @pl.when(y != q)
+        def _():
+            yb_copy(q, (q + NY - y) % NY, q).start()
+
+    for q in range(4):
+        @pl.when(x == q)
+        def _():
+            span = COUNT_X[q]
+            total = half[FIRST_X[q]:FIRST_X[q] + span]
             for d in (1, 3, 2):
-                remote(
-                    half.at[pl.ds(FIRST[xx], span)], from_x.at[d, pl.ds(0, span)],
-                    x_send.at[d], x_recv.at[d], dev_c(((xx + NX - d) % NX) * 2 + core),
-                ).wait_recv()
+                xa_copy(q, d, (q + NX - d) % NX).wait_recv()
                 total = total + from_x[d, 0:span]
-            quarter[0:span] = total
-
+            sum_a[0:span] = total
+
+    for q in range(4):
+        @pl.when(y == q)
+        def _():
+            span = COUNT_Y[q]
+            total = half[HALF + FIRST_Y[q]:HALF + FIRST_Y[q] + span]
+            for d in (1, 3, 2):
+                yb_copy(q, d, (q + NY - d) % NY).wait_recv()
+                total = total + from_y[d, 0:span]
+            sum_b[0:span] = total
+
+    skip = jnp.where(y == 3, 2, 0)
     holds = jnp.logical_or(x >= 2, y < 3)
 
-    def y_copy(d, yy, peer):
-        return remote(
-            quarter.at[yy], from_y.at[d], y_send.at[d], y_recv.at[d], dev_y(peer)
-        )
-
-    for d in range(1, NY):
+    def ya_copy(d, yy, peer):
+        return remote(sum_a.at[yy], from_y2.at[d], ya_send.at[d], ya_recv.at[d], dev_y(peer))
+
+    def xb_copy(d, spot, peer):
+        return remote(sum_b.at[spot], from_x2.at[d], xb_send.at[d], xb_recv.at[d], dev_x(peer))
+
+    for d in range(1, 4):
         yy = (y + d) % NY
+        xx = (x + d) % NX
 
         @pl.when(jnp.logical_or(x >= 2, yy < 3))
         def _():
-            y_copy(d, yy, yy).start()
-
-    def z_copy(d, zz, peer):
-        return remote(
-            block.at[pl.ds(zz * 8, 8)], from_z.at[d], z_send.at[d], z_recv.at[d], dev_z(peer)
+            ya_copy(d, yy, yy).start()
+
+        @pl.when(jnp.logical_or(xx >= 2, y < 3))
+        def _():
+            xb_copy(d, xx - skip, xx).start()
+
+    def zl_copy(d, spot, peer):
+        return remote(
+            block.at[pl.ds(spot * 32, 32)], from_zl.at[d],
+            zl_send.at[d], zl_recv.at[d], dev_z(zh, peer),
+        )
+
+    def zh_copy(d, spot, peer):
+        return remote(
+            from_zh.at[spot], from_zh.at[spot], zh_send.at[d], zh_recv.at[d], dev_z(peer, zl)
         )
 
     def zg_copy(d, spot, peer):
         return remote(
-            piece, line.at[pl.ds(spot * 8, 8)], zg_send.at[d], zg_recv.at[d], dev_z(peer)
-        )
-
-    def yg_copy(d, spot, peer):
-        return remote(
-            line, panel.at[spot], yg_send.at[d], yg_recv.at[d], dev_y(peer)
+            line.at[pl.ds(spot * 32, 32)], line.at[pl.ds(spot * 32, 32)],
+            zg_send.at[d], zg_recv.at[d], dev_z(zh, peer),
+        )
+
+    def gy_own(d, spot, peer):
+        return remote(line, own_ref.at[spot], gy_send.at[d], gy_recv.at[d], dev_y(peer))
+
+    def gy_head(d, spot, peer):
+        return remote(
+            line.at[pl.ds(0, ROWS)], out_a.at[core, x, spot],
+            gy_send.at[d], gy_recv.at[d], dev_y(peer),
+        )
+
+    def gx_head(d, spot, peer):
+        return remote(
+            line.at[pl.ds(ROWS, ROWS)], out_b.at[core, y, spot],
+            gx_send.at[d], gx_recv.at[d], dev_x(peer),
         )
 
     @pl.when(holds)
     def _():
-        total = quarter[y]
-        for d in range(1, NY):
-            y_copy(d, 0, (y + NY - d) % NY).wait_recv()
-            total = total + from_y[d]
-        block[...] = total
-        for d in range(1, nz):
-            zz = (z + d) % nz
-            z_copy(d, zz, zz).start()
-        total = block[pl.ds(pl.multiple_of(z * 8, 8), 8)]
-        for d in range(1, nz):
-            z_copy(d, 0, (z + nz - d) % nz).wait_recv()
-            total = total + from_z[d]
-        piece[...] = total
-        for d in range(1, nz):
-            zg_copy(d, z, (z + d) % nz).start()
-        line[pl.ds(pl.multiple_of(z * 8, 8), 8)] = total
-        for d in range(1, nz):
-            src = (z + nz - d) % nz
+        upper = sum_a[y]
+        lower = sum_b[x - skip]
+        for d in (1, 3, 2):
+            ya_copy(d, 0, (y + NY - d) % NY).wait_recv()
+            upper = upper + from_y2[d]
+        for d in (1, 3, 2):
+            xb_copy(d, 0, (x + NX - d) % NX).wait_recv()
+            lower = lower + from_x2[d]
+        block[0:ROWS] = upper
+        block[ROWS:BLK] = lower
+        for d in range(1, 4):
+            lo = (zl + d) % 4
+            zl_copy(d, lo, lo).start()
+        total = block[pl.ds(pl.multiple_of(zl * 32, 32), 32)]
+        for d in range(1, 4):
+            zl_copy(d, 0, (zl + 4 - d) % 4).wait_recv()
+            total = total + from_zl[d]
+        from_zh[zh] = total
+        for d in range(1, hops):
+            zh_copy(d, zh, (zh + d) % hops).start()
+        for d in range(1, hops):
+            src = (zh + hops - d) % hops
+            zh_copy(d, src, src).wait_recv()
+        total = from_zh[0]
+        for i in range(1, hops):
+            total = total + from_zh[i]
+        line[pl.ds(pl.multiple_of(zl * 32, 32), 32)] = total
+        for d in range(1, 4):
+            zg_copy(d, zl, (zl + d) % 4).start()
+        for d in range(1, 4):
+            src = (zl + 4 - d) % 4
             zg_copy(d, src, src).wait_recv()
-        for d in range(1, NY):
-            yg_copy(d, y, (y + d) % NY).start()
-        panel[y] = line[...]
-
-    for d in range(1, NY):
-        src = (y + NY - d) % NY
-
-        @pl.when(jnp.logical_or(x >= 2, src < 3))
-        def _():
-            yg_copy(d, src, src).wait_recv()
-
-    def xg_copy(d, xx, peer):
-        return remote(
-            panel.at[pl.ds(0, 3)], head_half.at[xx], xg_send.at[d], xg_recv.at[d],
-            dev_c(peer * 2 + core),
-        )
-
-    def cg_copy(xx):
-        return remote(
-            head_half.at[xx], head_ref.at[pl.ds((core * 2 + xx) * 3, 3)],
-            cg_send.at[xx], cg_recv.at[xx], dev_c(x * 2 + 1 - core),
+
+        @pl.when(x >= 2)
+        def _():
+            for d in range(1, 4):
+                gy_own(d, y, (y + d) % NY).start()
+            own_ref[y] = line[...]
+
+        @pl.when(x < 2)
+        def _():
+            for d in range(1, 4):
+                gy_head(d, y, (y + d) % NY).start()
+                gx_head(d, x, (x + d) % NX).start()
+            out_a[core, x, y] = line[0:ROWS]
+            out_b[core, y, x] = line[ROWS:BLK]
+
+    def hx_copy(d, xx, peer):
+        return remote(
+            out_a.at[core, xx], out_a.at[core, xx], hx_send.at[d], hx_recv.at[d], dev_x(peer)
+        )
+
+    def hy_copy(d, yy, peer):
+        return remote(
+            out_b.at[core, yy], out_b.at[core, yy], hy_send.at[d], hy_recv.at[d], dev_y(peer)
         )
 
     @pl.when(x < 2)
     def _():
-        for d in range(1, NX):
-            xg_copy(d, x, (x + d) % NX).start()
-        head_half[x] = panel[0:3]
-
-    for xx in range(2):
-        @pl.when(x != xx)
-        def _():
-            d = (x + NX - xx) % NX
-            xg_copy(d, xx, xx).wait_recv()
-
-        cg_copy(xx).start()
-        head_ref[pl.ds((core * 2 + xx) * 3, 3)] = head_half[xx]
+        for d in range(1, 4):
+            src = (y + NY - d) % NY
+
+            @pl.when(src < 3)
+            def _():
+                gy_head(d, src, src).wait_recv()
+
+        for d in range(1, 4):
+            hx_copy(d, x, (x + d) % NX).start()
+        own_ref[...] = jnp.zeros_like(own_ref)
+
+    @pl.when(y < 3)
+    def _():
+        for d in range(1, 4):
+            src = (x + NX - d) % NX
+
+            @pl.when(src < 2)
+            def _():
+                gx_head(d, src, src).wait_recv()
+
+        for d in range(1, 4):
+            hy_copy(d, y, (y + d) % NY).start()
+
+    def swap_a(half_core):
+        return remote(
+            out_a.at[half_core], out_a.at[half_core], cg_send.at[0], cg_recv.at[0],
+            dev_c(x * 2 + 1 - core),
+        )
+
+    def swap_b(half_core):
+        return remote(
+            out_b.at[half_core], out_b.at[half_core], cg_send.at[1], cg_recv.at[1],
+            dev_c(x * 2 + 1 - core),
+        )
+
+    for d in range(1, 4):
+        src = (y + NY - d) % NY
+
+        @pl.when(src < 3)
+        def _():
+            hy_copy(d, src, src).wait_recv()
+
+    swap_b(core).start()
+    for d in range(1, 4):
+        src = (x + NX - d) % NX
+
+        @pl.when(src < 2)
+        def _():
+            hx_copy(d, src, src).wait_recv()
+
+    swap_a(core).start()
 
     @pl.when(x >= 2)
     def _():
-        own_ref[...] = panel[...]
+        for d in range(1, 4):
+            src = (y + NY - d) % NY
+            gy_own(d, src, src).wait_recv()
+
+    swap_b(1 - core).wait_recv()
+    swap_a(1 - core).wait_recv()
+
+    for cp in sent:
+        cp.wait_send()
+    for q in range(4):
+        @pl.when(x != q)
+        def _():
+            xa_copy(q, (q + NX - x) % NX, q).wait_send()
+
+        @pl.when(y != q)
+        def _():
+            yb_copy(q, (q + NY - y) % NY, q).wait_send()
+
+    for d in range(1, 4):
+        yy = (y + d) % NY
+        xx = (x + d) % NX
+
+        @pl.when(jnp.logical_or(x >= 2, yy < 3))
+        def _():
+            ya_copy(d, yy, yy).wait_send()
+
+        @pl.when(jnp.logical_or(xx >= 2, y < 3))
+        def _():
+            xb_copy(d, xx - skip, xx).wait_send()
+
+    @pl.when(holds)
+    def _():
+        for d in range(1, 4):
+            lo = (zl + d) % 4
+            zl_copy(d, lo, lo).wait_send()
+            zg_copy(d, zl, lo).wait_send()
+        for d in range(1, hops):
+            zh_copy(d, zh, (zh + d) % hops).wait_send()
+
+        @pl.when(x >= 2)
+        def _():
+            for d in range(1, 4):
+                gy_own(d, y, (y + d) % NY).wait_send()
+
+        @pl.when(x < 2)
+        def _():
+            for d in range(1, 4):
+                gy_head(d, y, (y + d) % NY).wait_send()
+                gx_head(d, x, (x + d) % NX).wait_send()
 
     @pl.when(x < 2)
     def _():
-        own_ref[...] = jnp.zeros_like(own_ref)
-
-    for xx in range(2):
-        remote(
-            head_half.at[xx], head_ref.at[pl.ds(((1 - core) * 2 + xx) * 3, 3)],
-            cg_send.at[xx], cg_recv.at[xx], dev_c(x * 2 + 1 - core),
-        ).wait_recv()
-
-    for cp in sent:
-        cp.wait_send()
-    for xx in range(NX):
-        @pl.when(x != xx)
-        def _():
-            d = (xx + NX - x) % NX
-            remote(
-                half.at[pl.ds(FIRST[xx], COUNT[xx])], from_x.at[d, pl.ds(0, COUNT[xx])],
-                x_send.at[d], x_recv.at[d], dev_c(xx * 2 + core),
-            ).wait_send()
-    for d in range(1, NY):
-        yy = (y + d) % NY
-
-        @pl.when(jnp.logical_or(x >= 2, yy < 3))
-        def _():
-            y_copy(d, yy, yy).wait_send()
-
-    @pl.when(holds)
+        for d in range(1, 4):
+            hx_copy(d, x, (x + d) % NX).wait_send()
+
+    @pl.when(y < 3)
     def _():
-        for d in range(1, nz):
-            zz = (z + d) % nz
-            z_copy(d, zz, zz).wait_send()
-            zg_copy(d, z, zz).wait_send()
-        for d in range(1, NY):
-            yg_copy(d, y, (y + d) % NY).wait_send()
-
-    @pl.when(x < 2)
-    def _():
-        for d in range(1, NX):
-            xg_copy(d, x, (x + d) % NX).wait_send()
-    for xx in range(2):
-        cg_copy(xx).wait_send()
+        for d in range(1, 4):
+            hy_copy(d, y, (y + d) % NY).wait_send()
+
+    swap_b(core).wait_send()
+    swap_a(core).wait_send()
 
 
 def gram_everywhere(n_rows, base, field, grad, tile, kind):
     cells = field.shape[1]
-    nz = n_rows // NY
+    hops = n_rows // NY // 4
     f32 = jnp.float32
     vmem = pl.BlockSpec(memory_space=pltpu.VMEM)
-    dma = pltpu.SemaphoreType.DMA
-    blocks = lambda *lead: pltpu.VMEM(lead + (BLK, BLK), f32)
+    hbm = pl.BlockSpec(memory_space=pltpu.HBM)
+    pairs = [pltpu.SemaphoreType.DMA((4,))] * 2
+    halves = lambda *lead: pltpu.VMEM(lead + (ROWS, BLK), f32)
+    strip = lambda dtype: pltpu.VMEM((8, cells), dtype)
     return pl.pallas_call(
         functools.partial(gram_kernel, n_rows),
         out_shape=(
-            jax.ShapeDtypeStruct((12, BLK, BLK), f32),
+            jax.ShapeDtypeStruct((2, 2, 3, ROWS, BLK), f32),
+            jax.ShapeDtypeStruct((2, 3, 2, ROWS, BLK), f32),
             jax.ShapeDtypeStruct((4, BLK, BLK), f32),
         ),
-        in_specs=[pl.BlockSpec(memory_space=pl.ANY), vmem, vmem, vmem, vmem],
-        out_specs=(vmem, vmem),
+        in_specs=[hbm] * 5,
+        out_specs=(vmem, vmem, vmem),
         scratch_shapes=[
             pltpu.VMEM((8, cells, BLK), jnp.bfloat16),
             pltpu.VMEM((cells, 8 * BLK), jnp.bfloat16),
-            pltpu.VMEM((8, BLK), jnp.int32),
-            pltpu.VMEM((8, 8, BLK), jnp.int32),
-            pltpu.VMEM((8, cells), f32),
-            pltpu.VMEM((8, cells), f32),
-            blocks(2 * HALF), blocks(HALF), blocks(HALF), blocks(NX, 4), blocks(4),
-            blocks(NY), blocks(), pltpu.VMEM((nz, 8, BLK), f32), pltpu.VMEM((8, BLK), f32),
-            blocks(), blocks(4), blocks(2, 3),
-            dma((8,)), dma((8,)), dma((8,)), dma((8,)), dma((2,)), dma((2,)),
-            dma((2,)), dma((NX,)), dma((NX,)), dma((NY,)), dma((NY,)), dma((nz,)), dma((nz,)),
-            dma((nz,)), dma((nz,)), dma((NY,)), dma((NY,)), dma((NX,)), dma((NX,)),
-            dma((2,)), dma((2,)),
+            strip(f32), strip(jnp.bfloat16),
+            pltpu.VMEM((1, BLK), jnp.int32), pltpu.VMEM((1, BLK), jnp.int32),
+            pltpu.VMEM((8, BLK), jnp.int32), pltpu.VMEM((8, 8, BLK), jnp.int32),
+            strip(f32), strip(f32),
+            halves(2, 2 * HALF), halves(2 * HALF), halves(2 * HALF),
+            halves(4, 4), halves(4, 4), halves(4), halves(4), halves(4), halves(4),
+            pltpu.VMEM((BLK, BLK), f32), pltpu.VMEM((4, 32, BLK), f32),
+            pltpu.VMEM((hops, 32, BLK), f32), pltpu.VMEM((BLK, BLK), f32),
+            pltpu.SemaphoreType.DMA((4,)),
+            *[pltpu.SemaphoreType.DMA((8,))] * 4,
+            pltpu.SemaphoreType.DMA((2,)), pltpu.SemaphoreType.DMA((2,)),
+            pltpu.SemaphoreType.DMA((2,)),
+            *pairs * 4, *pairs, *pairs, *pairs, *pairs * 4,
+            pltpu.SemaphoreType.DMA((2,)), pltpu.SemaphoreType.DMA((2,)),
         ],
         compiler_params=pltpu.CompilerParams(
             collective_id=0, has_side_effects=True, vmem_limit_bytes=48 << 20
         ),
         name="gram",
-    )(base, field, grad, tile, kind)
+    )(*[pltpu.with_memory_space_constraint(v, pltpu.HBM) for v in (base, field, grad, tile, kind)])
 
 
 def dot_f32(left, right, dims=((1,), (0,))):
@@ -472,12 +623,16 @@
             work[low:BLK, :] = work[low:BLK, :] - dot_f32(done[:, low:BLK], done, ((0,), (0,)))
 
 
-def factor_kernel(head_ref, own_ref, r_ref, m_ref, mat, work, scaled, inv):
+def factor_kernel(head_a, head_b, own_ref, r_ref, m_ref, mat, head_ref, work, scaled, inv):
     c = lax.axis_index("cols")
     eye = (
         lax.broadcasted_iota(jnp.int32, (BLK, BLK), 0)
         == lax.broadcasted_iota(jnp.int32, (BLK, BLK), 1)
     ).astype(jnp.float32)
+    for spot in range(12):
+        k, at_x, at_y = spot // 6, spot // 3 % 2, spot % 3
+        head_ref[spot, 0:ROWS] = head_a[k, at_x, at_y]
+        head_ref[spot, ROWS:BLK] = head_b[k, at_y, at_x]
     near = jnp.minimum(c, 3)
     for k in range(4):
         for j in range(k, 4):
@@ -508,7 +663,7 @@
         m_ref[k:k + 1, :] = solved[k].T[0:1, :]
 
 
-def factor_and_solve(head, own):
+def factor_and_solve(head_a, head_b, own):
     f32 = jnp.float32
     vmem = pl.BlockSpec(memory_space=pltpu.VMEM)
     return pl.pallas_call(
@@ -517,25 +672,26 @@
             jax.ShapeDtypeStruct((512, BLK), f32),
             jax.ShapeDtypeStruct((4, BLK), f32),
         ),
-        in_specs=[vmem, vmem],
+        in_specs=[vmem, vmem, vmem],
         out_specs=(vmem, vmem),
         scratch_shapes=[
             pltpu.VMEM((4, BLK, 768), f32),
+            pltpu.VMEM((12, BLK, BLK), f32),
             pltpu.VMEM((BLK, 2 * BLK), f32),
             pltpu.VMEM((BLK, 2 * BLK), f32),
             pltpu.VMEM((4, BLK, BLK), f32),
         ],
         compiler_params=pltpu.CompilerParams(vmem_limit_bytes=48 << 20),
         name="factor",
-    )(head, own)
+    )(head_a, head_b, own)
 
 
 def shards(n_rows, sens_base, design_field, gradient, tile_index, type_codes):
-    head, own = gram_everywhere(
+    head_a, head_b, own = gram_everywhere(
         n_rows, sens_base, design_field, gradient,
         tile_index.reshape(1, BLK), type_codes.reshape(1, BLK),
     )
-    r_panels, multipliers = factor_and_solve(head, own)
+    r_panels, multipliers = factor_and_solve(head_a, head_b, own)
     return r_panels, multipliers.reshape(-1)
 
 

time: 123 us -> 108 us (0.88)
  Pallas kernels: 117 us -> 107 us
  local copies, waits for them, and re-layouts: 4.37 us -> 0 us
    pallas_call x1, Pallas kernels: 93.8 us -> 83.8 us  [gram_everywhere(): pl.pallas_call(functools.partial(gram_kernel, n_rows), out_shape=(jax.Sha...]
    unnamed x10 -> x0, local copies, waits for them, and re-layouts: 4.37 us -> none
where the time goes in v2:
time: 108 us
  Pallas kernels  107 us (99%)
    pallas_call x1, Pallas kernels, gram_everywhere(): pl.pallas_call(functools.partial(gram_kernel, n_rows), out_shape=(jax.Sha...  83.8 us
    pallas_call x1, Pallas kernels, factor_and_solve(): pl.pallas_call(factor_kernel, out_shape=(jax.ShapeDtypeStruct((512, BLK),...  23.5 us

profile of v2, /device:TPU:1, one launch (start us, length us, event | category | flops | bytes accessed | tf_op | source)
XLA Modules:
  0.0 108.0 jit_solution(17541992019780124916)
XLA Ops:
  0.6 83.8 %gram.1 = (f32[2,2,3,64,128]{4,3,2,1,0:T(8,128)S(1)}, f32[2,3,2,64,128]{4,3,2,1,0:T(8,128)S(1)}, f32[4,128,128]{2,1,0:T(8,128)S(1)}) custom-call(bf16[8192,128]{1,0:T(8,128)(2,1)} %base_ref.1, f32[8,1024]{1,0:T(8,128)} %field_hbm.1, bf16[8,1024]{1,0:T(8,128)(2,1)} %grad_hbm.1, s32[1,128]{1,0:T(1,128)} %bitcast.3, s32[1,128]{1,0:T(1,128)} %bitcast.4), custom_call_target="tpu_custom_call" | custom-call | tf_op jit(solution)/shard_map/gram/pallas_call | solution.py:523
  84.5 23.5 %factor.1 = (f32[512,128]{1,0:T(8,128)}, f32[4,128]{1,0:T(4,128)}) custom-call(f32[2,2,3,64,128]{4,3,2,1,0:T(8,128)S(1)} %get-tuple-element.7.head_a, f32[2,3,2,64,128]{4,3,2,1,0:T(8,128)S(1)} %get-tuple-element.8.head_b, f32[4,128,128]{2,1,0:T(8,128)S(1)} %get-tuple-element.9.own_ref), custom_call_target="tpu_custom_call" | custom-call | tf_op jit(solution)/shard_map/factor/pallas_call | solution.py:669

commit v3 on v2

--- a/solution.py
+++ b/solution.py
@@ -568,59 +568,60 @@
     return jnp.broadcast_to(vec[row:row + 1, :], (8, BLK))
 
 
-def eliminate_8(rows8, start):
-    cols = [across(rows8, start + t) for t in range(8)]
-    entry = [[along(cols[t], s) if t <= s else None for t in range(8)] for s in range(8)]
-    inverse = [[None] * 8 for _ in range(8)]
-    recip = []
-    for t in range(8):
-        recip.append(1.0 / entry[t][t])
-        for s in range(t + 1, 8):
-            factor = entry[s][t] * recip[t]
-            for u in range(t + 1, s + 1):
-                entry[s][u] = entry[s][u] - factor * entry[u][t]
-            for u in range(t):
-                inverse[s][u] = inverse[s][u] - factor * inverse[t][u]
-            inverse[s][t] = -factor
-    return inverse, recip
+def split_3(x):
+    high = x.astype(jnp.bfloat16)
+    rest = x - high.astype(jnp.float32)
+    mid = rest.astype(jnp.bfloat16)
+    return high, mid, (rest - mid.astype(jnp.float32)).astype(jnp.bfloat16)
+
+
+def outer(left, right):
+    lh, lm, ll = split_3(left)
+    rh, rm, rl = split_3(right)
+    return lax.dot_general(
+        jnp.concatenate([lh, lh, lm, lm, lh, ll], axis=0),
+        jnp.concatenate([rh, rm, rh, rm, rl, rh], axis=0),
+        (((0,), (0,)), ((), ())), preferred_element_type=jnp.float32,
+    )
 
 
 def factor_block(work, scaled):
     rows = lax.broadcasted_iota(jnp.int32, (8, BLK), 0)
-    for q in range(4):
-        at = [32 * q + 8 * s for s in range(4)]
+    tall = 64
+    for q in range(BLK // tall):
+        at = [tall * q + 8 * s for s in range(tall // 8)]
         xa = [work[a:a + 8, 0:BLK] for a in at]
         xe = [work[a:a + 8, BLK:2 * BLK] for a in at]
-        for s in range(4):
-            inverse, recip = eliminate_8(xa[s], at[s])
-            new_a, new_e = xa[s], xe[s]
-            for t in range(7):
-                col = jnp.zeros((8, BLK), jnp.float32)
-                for u in range(t + 1, 8):
-                    col = jnp.where(rows == u, inverse[u][t], col)
-                new_a = new_a + col * along(xa[s], t)
-                new_e = new_e + col * along(xe[s], t)
-            scale = recip[0]
-            for u in range(1, 8):
-                scale = jnp.where(rows == u, recip[u], scale)
-            scale = jnp.sqrt(scale)
-            scaled[at[s]:at[s] + 8, 0:BLK] = new_a * scale
-            scaled[at[s]:at[s] + 8, BLK:2 * BLK] = new_e * scale
-            row_a = [along(new_a, t) for t in range(8)] if s < 3 else None
-            row_e = [along(new_e, t) for t in range(8)] if s < 3 else None
-            for later in range(s + 1, 4):
-                cols = [across(xa[later], at[s] + u) for u in range(8)]
-                for t in range(8):
-                    mult = cols[t]
-                    for u in range(t):
-                        mult = mult + cols[u] * inverse[t][u]
-                    mult = mult * recip[t]
-                    xa[later] = xa[later] - mult * row_a[t]
-                    xe[later] = xe[later] - mult * row_e[t]
-        if q < 3:
-            low = 32 * (q + 1)
-            done = scaled[32 * q:low, :]
-            work[low:BLK, :] = work[low:BLK, :] - dot_f32(done[:, low:BLK], done, ((0,), (0,)))
+        for s in range(len(at)):
+            cols = [across(xa[s], at[s] + t) for t in range(8)]
+            below = {n: [across(xa[n], at[s] + t) for t in range(8)]
+                     for n in range(s + 1, len(at))}
+            pivots = None
+            for t in range(8):
+                entry = {u: along(cols[t], u) for u in range(t, 8)}
+                pivots = entry[t] if pivots is None else jnp.where(rows >= t, entry[t], pivots)
+                recip = 1.0 / entry[t]
+                row_a, row_e = along(xa[s], t), along(xe[s], t)
+                if t < 7:
+                    mult = cols[t] * recip
+                    for u in range(t + 1, 8):
+                        cols[u] = cols[u] - mult * entry[u]
+                    mult = jnp.where(rows > t, mult, 0.0)
+                    xa[s] = xa[s] - mult * row_a
+                    xe[s] = xe[s] - mult * row_e
+                for n in below:
+                    mult = below[n][t] * recip
+                    for u in range(t + 1, 8):
+                        below[n][u] = below[n][u] - mult * entry[u]
+                    xa[n] = xa[n] - mult * row_a
+                    xe[n] = xe[n] - mult * row_e
+            scale = 1.0 / jnp.sqrt(pivots)
+            scaled[at[s]:at[s] + 8, 0:BLK] = xa[s] * scale
+            scaled[at[s]:at[s] + 8, BLK:2 * BLK] = xe[s] * scale
+        low = tall * (q + 1)
+        if low < BLK:
+            done = scaled[tall * q:low, :]
+            work[low:BLK, :] = work[low:BLK, :] - outer(done[:, low:BLK], done)
 
 
 def factor_kernel(head_a, head_b, own_ref, r_ref, m_ref, mat, head_ref, work, scaled, inv):
@@ -647,20 +648,33 @@
         work[:, BLK:2 * BLK] = eye
         factor_block(work, scaled)
         low = (k + 1) * BLK
-        inv[k] = scaled[:, BLK:2 * BLK]
-        mat[k, :, low:768] = dot_f32(scaled[:, BLK:2 * BLK], mat[k, :, low:768])
+        inverse = scaled[:, BLK:2 * BLK]
+        inv[k] = inverse
+        if k == 3:
+            mat[k, :, low:768] = dot_f32(inverse, mat[k, :, low:768])
+            r_ref[k * BLK:(k + 1) * BLK, :] = mat[k, :, 512:640]
+            continue
+        near_cols = dot_f32(inverse, mat[k, :, low:low + BLK])
+        mat[k, :, low:low + BLK] = near_cols
+        mat[k + 1, :, low:low + BLK] = mat[k + 1, :, low:low + BLK] - dot_f32(
+            near_cols, near_cols, ((0,), (0,))
+        )
+        far = low + BLK
+        mat[k, :, far:768] = dot_f32(inverse, mat[k, :, far:768])
         r_ref[k * BLK:(k + 1) * BLK, :] = mat[k, :, 512:640]
-        for i in range(k + 1, 4):
+        mat[k + 1, :, far:768] = mat[k + 1, :, far:768] - dot_f32(
+            near_cols, mat[k, :, far:768], ((0,), (0,))
+        )
+        for i in range(k + 2, 4):
             mat[i, :, i * BLK:768] = mat[i, :, i * BLK:768] - dot_f32(
                 mat[k, :, i * BLK:(i + 1) * BLK], mat[k, :, i * BLK:768], ((0,), (0,))
             )
-    solved = [None] * 4
+    rest = [mat[k, :, 640:768] for k in range(4)]
     for k in (3, 2, 1, 0):
-        rest = mat[k, :, 640:768]
-        for i in range(k + 1, 4):
-            rest = rest - dot_f32(mat[k, :, i * BLK:(i + 1) * BLK], solved[i])
-        solved[k] = dot_f32(inv[k], rest, ((0,), (0,)))
-        m_ref[k:k + 1, :] = solved[k].T[0:1, :]
+        solved = dot_f32(inv[k], rest[k], ((0,), (0,)))
+        for i in range(k):
+            rest[i] = rest[i] - dot_f32(mat[i, :, k * BLK:(k + 1) * BLK], solved)
+        m_ref[k:k + 1, :] = solved.T[0:1, :]
 
 
 def factor_and_solve(head_a, head_b, own):

time: 108 us -> 104 us (0.963)
  Pallas kernels: 107 us -> 103 us
    pallas_call x1, Pallas kernels: 23.5 us -> 19 us  [factor_and_solve(): pl.pallas_call(factor_kernel, out_shape=(jax.ShapeDtypeStruct((512, BLK),...]
where the time goes in v3:
time: 104 us; the launch traced here: 103 us
  Pallas kernels  103 us (99%)
    pallas_call x1, Pallas kernels, gram_everywhere(): pl.pallas_call(functools.partial(gram_kernel, n_rows), out_shape=(jax.Sha...  83.8 us
    pallas_call x1, Pallas kernels, factor_and_solve(): pl.pallas_call(factor_kernel, out_shape=(jax.ShapeDtypeStruct((512, BLK),...  19 us

profile of v3, /device:TPU:1, one launch (start us, length us, event | category | flops | bytes accessed | tf_op | source)
XLA Modules:
  0.0 103.4 jit_solution(11574122107733491593)
XLA Ops:
  0.6 83.8 %gram.1 = (f32[2,2,3,64,128]{4,3,2,1,0:T(8,128)S(1)}, f32[2,3,2,64,128]{4,3,2,1,0:T(8,128)S(1)}, f32[4,128,128]{2,1,0:T(8,128)S(1)}) custom-call(bf16[8192,128]{1,0:T(8,128)(2,1)} %base_ref.1, f32[8,1024]{1,0:T(8,128)} %field_hbm.1, bf16[8,1024]{1,0:T(8,128)(2,1)} %grad_hbm.1, s32[1,128]{1,0:T(1,128)} %bitcast.3, s32[1,128]{1,0:T(1,128)} %bitcast.4), custom_call_target="tpu_custom_call" | custom-call | tf_op jit(solution)/shard_map/gram/pallas_call | solution.py:523
  84.5 19.0 %factor.1 = (f32[512,128]{1,0:T(8,128)}, f32[4,128]{1,0:T(4,128)}) custom-call(f32[2,2,3,64,128]{4,3,2,1,0:T(8,128)S(1)} %get-tuple-element.7.head_a, f32[2,3,2,64,128]{4,3,2,1,0:T(8,128)S(1)} %get-tuple-element.8.head_b, f32[4,128,128]{2,1,0:T(8,128)S(1)} %get-tuple-element.9.own_ref), custom_call_target="tpu_custom_call" | custom-call | tf_op jit(solution)/shard_map/factor/pallas_call | solution.py:683

commit v4 on v3

--- a/solution.py
+++ b/solution.py
@@ -76,14 +76,14 @@
     def greet(device):
         pl.semaphore_signal(barrier, inc=1, device_id=device, device_id_type=MESH)
 
+    for d in range(1, hops):
+        greet(dev_z((zh + d) % hops, zl))
     for d in range(1, 8):
         greet(dev_c((c + d) % 8))
     for d in range(1, NY):
         greet(dev_y((y + d) % NY))
     for d in range(1, 4):
         greet(dev_z(zh, (zl + d) % 4))
-    for d in range(1, hops):
-        greet(dev_z((zh + d) % hops, zl))
     greet((up, c))
     greet((down, c))
     loads = []
@@ -585,51 +585,65 @@
     )
 
 
-def factor_block(work, scaled):
+def factor_block(work, inv):
     rows = lax.broadcasted_iota(jnp.int32, (8, BLK), 0)
+    lane = lax.broadcasted_iota(jnp.int32, (8, BLK), 1)
     tall = 64
     for q in range(BLK // tall):
         at = [tall * q + 8 * s for s in range(tall // 8)]
-        xa = [work[a:a + 8, 0:BLK] for a in at]
-        xe = [work[a:a + 8, BLK:2 * BLK] for a in at]
+        xs = [work[a:a + 8, :] for a in at]
+        ahead = None
         for s in range(len(at)):
-            cols = [across(xa[s], at[s] + t) for t in range(8)]
-            below = {n: [across(xa[n], at[s] + t) for t in range(8)]
-                     for n in range(s + 1, len(at))}
-            pivots = None
+            start = at[s]
+            cols = ahead or [across(xs[s], start + t) for t in range(8)]
+            later = range(s + 1, len(at))
+            below = {n: [across(xs[n], start + t) for t in range(8)] for n in later}
+            ahead = [across(xs[s + 1], at[s + 1] + t) for t in range(8)] if later else None
+            here = jnp.logical_and(lane >= start, lane < start + 8)
+            xs[s] = jnp.where(here, jnp.where(lane - start == rows, 1.0, 0.0), xs[s])
+            for n in later:
+                xs[n] = jnp.where(here, 0.0, xs[n])
+            pivot = along(cols[0], 0)
+            pivots = pivot
             for t in range(8):
-                entry = {u: along(cols[t], u) for u in range(t, 8)}
-                pivots = entry[t] if pivots is None else jnp.where(rows >= t, entry[t], pivots)
-                recip = 1.0 / entry[t]
-                row_a, row_e = along(xa[s], t), along(xe[s], t)
+                entry = {u: along(cols[t], u) for u in range(t + 1, 8)}
+                recip = 1.0 / pivot
+                row = along(xs[s], t)
                 if t < 7:
+                    pivot = along(cols[t + 1], t + 1) - (entry[t + 1] * recip) * entry[t + 1]
+                    pivots = jnp.where(rows >= t + 1, pivot, pivots)
                     mult = cols[t] * recip
                     for u in range(t + 1, 8):
                         cols[u] = cols[u] - mult * entry[u]
-                    mult = jnp.where(rows > t, mult, 0.0)
-                    xa[s] = xa[s] - mult * row_a
-                    xe[s] = xe[s] - mult * row_e
-                for n in below:
+                    xs[s] = xs[s] - jnp.where(rows > t, mult, 0.0) * row
+                for n in later:
                     mult = below[n][t] * recip
+                    if n == s + 1:
+                        for u in range(8):
+                            ahead[u] = ahead[u] - mult * along(below[n][t], u)
                     for u in range(t + 1, 8):
                         below[n][u] = below[n][u] - mult * entry[u]
-                    xa[n] = xa[n] - mult * row_a
-                    xe[n] = xe[n] - mult * row_e
-            scale = 1.0 / jnp.sqrt(pivots)
-            scaled[at[s]:at[s] + 8, 0:BLK] = xa[s] * scale
-            scaled[at[s]:at[s] + 8, BLK:2 * BLK] = xe[s] * scale
+                    xs[n] = xs[n] - mult * row
+            inv[start:start + 8, :] = xs[s] * (1.0 / jnp.sqrt(pivots))
         low = tall * (q + 1)
         if low < BLK:
-            done = scaled[tall * q:low, :]
-            work[low:BLK, :] = work[low:BLK, :] - outer(done[:, low:BLK], done)
-
-
-def factor_kernel(head_a, head_b, own_ref, r_ref, m_ref, mat, head_ref, work, scaled, inv):
+            done = inv[tall * q:low, :]
+            row_at = lax.broadcasted_iota(jnp.int32, done.shape, 0) + tall * q
+            col_at = lax.broadcasted_iota(jnp.int32, done.shape, 1)
+            past = jnp.where(jnp.logical_and(col_at < low, col_at > row_at), 0.0, done)
+            rest = work[low:BLK, :]
+            col_at = lax.broadcasted_iota(jnp.int32, rest.shape, 1)
+            rest = jnp.where(jnp.logical_and(col_at >= tall * q, col_at < low), 0.0, rest)
+            work[low:BLK, :] = rest - outer(done[:, low:BLK], past)
+    lower = (
+        lax.broadcasted_iota(jnp.int32, (BLK, BLK), 0)
+        >= lax.broadcasted_iota(jnp.int32, (BLK, BLK), 1)
+    )
+    inv[...] = jnp.where(lower, inv[...], 0.0)
+
+
+def factor_kernel(head_a, head_b, own_ref, r_ref, m_ref, mat, head_ref, work, inv):
     c = lax.axis_index("cols")
-    eye = (
-        lax.broadcasted_iota(jnp.int32, (BLK, BLK), 0)
-        == lax.broadcasted_iota(jnp.int32, (BLK, BLK), 1)
-    ).astype(jnp.float32)
     for spot in range(12):
         k, at_x, at_y = spot // 6, spot // 3 % 2, spot % 3
         head_ref[spot, 0:ROWS] = head_a[k, at_x, at_y]
@@ -644,12 +658,10 @@
         mat[k, :, 512:640] = jnp.where(c >= 4, own_ref[k], found)
         mat[k, :, 640:768] = jnp.broadcast_to(head_ref[len(HEAD), k:k + 1, :], (BLK, BLK)).T
     for k in range(4):
-        work[:, 0:BLK] = mat[k, :, k * BLK:(k + 1) * BLK]
-        work[:, BLK:2 * BLK] = eye
-        factor_block(work, scaled)
+        work[...] = mat[k, :, k * BLK:(k + 1) * BLK]
+        factor_block(work, inv.at[k])
         low = (k + 1) * BLK
-        inverse = scaled[:, BLK:2 * BLK]
-        inv[k] = inverse
+        inverse = inv[k]
         if k == 3:
             mat[k, :, low:768] = dot_f32(inverse, mat[k, :, low:768])
             r_ref[k * BLK:(k + 1) * BLK, :] = mat[k, :, 512:640]
@@ -691,8 +703,7 @@
         scratch_shapes=[
             pltpu.VMEM((4, BLK, 768), f32),
             pltpu.VMEM((12, BLK, BLK), f32),
-            pltpu.VMEM((BLK, 2 * BLK), f32),
-            pltpu.VMEM((BLK, 2 * BLK), f32),
+            pltpu.VMEM((BLK, BLK), f32),
             pltpu.VMEM((4, BLK, BLK), f32),
         ],
         compiler_params=pltpu.CompilerParams(vmem_limit_bytes=48 << 20),

time: 104 us -> 99.2 us (0.954)
  Pallas kernels: 103 us -> 98.4 us
    pallas_call x1, Pallas kernels: 19 us -> 14.5 us  [factor_and_solve(): pl.pallas_call(factor_kernel, out_shape=(jax.ShapeDtypeStruct((512, BLK),...]
where the time goes in v4:
time: 99.2 us; the launch traced here: 99 us
  Pallas kernels  98.4 us (99%)
    pallas_call x1, Pallas kernels, gram_everywhere(): pl.pallas_call(functools.partial(gram_kernel, n_rows), out_shape=(jax.Sha...  83.9 us
    pallas_call x1, Pallas kernels, factor_and_solve(): pl.pallas_call(factor_kernel, out_shape=(jax.ShapeDtypeStruct((512, BLK),...  14.5 us

profile of v4, /device:TPU:1, one launch (start us, length us, event | category | flops | bytes accessed | tf_op | source)
XLA Modules:
  0.0 99.0 jit_solution(6615952241362578197)
XLA Ops:
  0.6 83.9 %gram.1 = (f32[2,2,3,64,128]{4,3,2,1,0:T(8,128)S(1)}, f32[2,3,2,64,128]{4,3,2,1,0:T(8,128)S(1)}, f32[4,128,128]{2,1,0:T(8,128)S(1)}) custom-call(bf16[8192,128]{1,0:T(8,128)(2,1)} %base_ref.1, f32[8,1024]{1,0:T(8,128)} %field_hbm.1, bf16[8,1024]{1,0:T(8,128)(2,1)} %grad_hbm.1, s32[1,128]{1,0:T(1,128)} %bitcast.3, s32[1,128]{1,0:T(1,128)} %bitcast.4), custom_call_target="tpu_custom_call" | custom-call | tf_op jit(solution)/shard_map/gram/pallas_call | solution.py:523
  84.5 14.5 %factor.1 = (f32[512,128]{1,0:T(8,128)}, f32[4,128]{1,0:T(4,128)}) custom-call(f32[2,2,3,64,128]{4,3,2,1,0:T(8,128)S(1)} %get-tuple-element.7.head_a, f32[2,3,2,64,128]{4,3,2,1,0:T(8,128)S(1)} %get-tuple-element.8.head_b, f32[4,128,128]{2,1,0:T(8,128)S(1)} %get-tuple-element.9.own_ref), custom_call_target="tpu_custom_call" | custom-call | tf_op jit(solution)/shard_map/factor/pallas_call | solution.py:695

commit v5 on v4

--- a/solution.py
+++ b/solution.py
@@ -12,7 +12,6 @@
 NX = 4
 NY = 4
 MESH = pl.DeviceIdType.MESH
-HIGHEST = lax.Precision.HIGHEST
 HEAD = [(a, b) for a in range(4) for b in range(a, 4)]
 COUNT_X = (3, 3, 4, 4)
 FIRST_X = (0, 3, 6, 10)
@@ -20,6 +19,7 @@
 FIRST_Y = (0, 4, 8, 12)
 HALF = 14
 ROWS = BLK // 2
+PARTS = 2
 
 
 def slot_of(core, x, y):
@@ -112,14 +112,20 @@
     cp = remote(field_ref, south, halo_send.at[1], halo_recv.at[1], (up, c))
     cp.start()
     sent.append(cp)
-    for d in (4, 3, 5, 2, 6, 1, 7):
-        to = (c + d) % 8
-        cp = remote(
-            base_ref.at[pl.ds(to * cells, cells), :], raw.at[c],
-            a2a_send.at[d], a2a_recv.at[d], dev_c(to),
-        )
-        cp.start()
-        sent.append(cp)
+    part = cells // PARTS
+
+    def a2a_copy(h, d, spot, peer):
+        return remote(
+            base_ref.at[pl.ds(peer * cells + h * part, part), :],
+            raw.at[spot, pl.ds(h * part, part)],
+            a2a_send.at[h * 8 + d], a2a_recv.at[h * 8 + d], dev_c(peer),
+        )
+
+    for h in range(PARTS):
+        for d in (4, 3, 5, 2, 6, 1, 7):
+            cp = a2a_copy(h, d, c, (c + d) % 8)
+            cp.start()
+            sent.append(cp)
     mine = pltpu.make_async_copy(
         base_ref.at[pl.ds(c * cells, cells), :], raw.at[c], a2a_recv.at[0]
     )
@@ -172,25 +178,6 @@
         src = (c + 8 - d) % 8
         remote(codes_mine, codes.at[src], code_send.at[d], code_recv.at[d], dev_c(src)).wait_recv()
 
-    for cs in range(8):
-        @pl.when(c == cs)
-        def _():
-            mine.wait()
-
-        @pl.when(c != cs)
-        def _():
-            d = (c + 8 - cs) % 8
-            remote(
-                base_ref.at[pl.ds(0, cells), :], raw.at[cs],
-                a2a_send.at[d], a2a_recv.at[d], dev_c(cs),
-            ).wait_recv()
-
-        chosen = jnp.logical_and(
-            kind_of == codes[cs, 1:2, :], tile_of == codes[cs, 0:1, :]
-        ).astype(jnp.float32).astype(jnp.bfloat16)
-        added = jnp.dot(spread_t, chosen, preferred_element_type=jnp.float32)
-        jac[:, cs * BLK:(cs + 1) * BLK] = (raw[cs].astype(jnp.float32) + added).astype(jnp.bfloat16)
-
     where = {}
     for k in range(2):
         for xx in range(NX):
@@ -198,24 +185,44 @@
                 low = FIRST_Y[yy] + (xx if yy < 3 else xx - 2)
                 where[slot_of(k, xx, yy)] = (k, FIRST_X[xx] + yy, HALF + low)
 
-    def put(key, value):
+    def put(key, value, add=False):
         k, upper, lower = where[key]
-        parts[k, upper] = value[0:ROWS]
-        parts[k, lower] = value[ROWS:BLK]
+        parts[k, upper] = value[0:ROWS] + (parts[k, upper] if add else 0.0)
+        parts[k, lower] = value[ROWS:BLK] + (parts[k, lower] if add else 0.0)
 
     contract = (((0,), (0,)), ((), ()))
-    for pa in range(2):
-        left = jac[:, pa * 256:(pa + 1) * 256]
-        for pb in range(pa, 4):
-            prod = lax.dot_general(
-                left, jac[:, pb * 256:(pb + 1) * 256], contract,
-                preferred_element_type=jnp.float32,
-            )
-            for i in range(2):
-                for j in range(2):
-                    key = (pa * 2 + i, pb * 2 + j)
-                    if key in where:
-                        put(key, prod[i * BLK:(i + 1) * BLK, j * BLK:(j + 1) * BLK])
+    for h in range(PARTS):
+        for cs in range(8):
+            if h == 0:
+                @pl.when(c == cs)
+                def _():
+                    mine.wait()
+
+            @pl.when(c != cs)
+            def _():
+                a2a_copy(h, (c + 8 - cs) % 8, cs, cs).wait_recv()
+
+            chosen = jnp.logical_and(
+                kind_of == codes[cs, 1:2, :], tile_of == codes[cs, 0:1, :]
+            ).astype(jnp.float32).astype(jnp.bfloat16)
+            span = slice(h * part, (h + 1) * part)
+            added = jnp.dot(spread_t[span], chosen, preferred_element_type=jnp.float32)
+            jac[span, cs * BLK:(cs + 1) * BLK] = (
+                raw[cs, span].astype(jnp.float32) + added
+            ).astype(jnp.bfloat16)
+
+        for pa in range(2):
+            left = jac[span, pa * 256:(pa + 1) * 256]
+            for pb in range(pa, 4):
+                prod = lax.dot_general(
+                    left, jac[span, pb * 256:(pb + 1) * 256], contract,
+                    preferred_element_type=jnp.float32,
+                )
+                for i in range(2):
+                    for j in range(2):
+                        key = (pa * 2 + i, pb * 2 + j)
+                        if key in where:
+                            put(key, prod[i * BLK:(i + 1) * BLK, j * BLK:(j + 1) * BLK], h > 0)
     loads[3].wait()
     proj = jnp.dot(grad_ref[...], jac[:, 0:512], preferred_element_type=jnp.float32)
     proj = jnp.sum(
@@ -541,7 +548,7 @@
             pltpu.VMEM((BLK, BLK), f32), pltpu.VMEM((4, 32, BLK), f32),
             pltpu.VMEM((hops, 32, BLK), f32), pltpu.VMEM((BLK, BLK), f32),
             pltpu.SemaphoreType.DMA((4,)),
-            *[pltpu.SemaphoreType.DMA((8,))] * 4,
+            *[pltpu.SemaphoreType.DMA((8 * PARTS,))] * 2, *[pltpu.SemaphoreType.DMA((8,))] * 2,
             pltpu.SemaphoreType.DMA((2,)), pltpu.SemaphoreType.DMA((2,)),
             pltpu.SemaphoreType.DMA((2,)),
             *pairs * 4, *pairs, *pairs, *pairs, *pairs * 4,
@@ -554,12 +561,6 @@
     )(*[pltpu.with_memory_space_constraint(v, pltpu.HBM) for v in (base, field, grad, tile, kind)])
 
 
-def dot_f32(left, right, dims=((1,), (0,))):
-    return lax.dot_general(
-        left, right, (dims, ((), ())), precision=HIGHEST, preferred_element_type=jnp.float32
-    )
-
-
 def across(vec, col):
     return jnp.broadcast_to(vec[:, col:col + 1], (8, BLK))
 
@@ -575,13 +576,13 @@
     return high, mid, (rest - mid.astype(jnp.float32)).astype(jnp.bfloat16)
 
 
-def outer(left, right):
+def dot_f32(left, right, dims=((1,), (0,))):
     lh, lm, ll = split_3(left)
     rh, rm, rl = split_3(right)
     return lax.dot_general(
-        jnp.concatenate([lh, lh, lm, lm, lh, ll], axis=0),
-        jnp.concatenate([rh, rm, rh, rm, rl, rh], axis=0),
-        (((0,), (0,)), ((), ())), preferred_element_type=jnp.float32,
+        jnp.concatenate([lh, lh, lm, lm, lh, ll], axis=dims[0][0]),
+        jnp.concatenate([rh, rm, rh, rm, rl, rh], axis=dims[1][0]),
+        (dims, ((), ())), preferred_element_type=jnp.float32,
     )
 
 
@@ -634,7 +635,7 @@
             rest = work[low:BLK, :]
             col_at = lax.broadcasted_iota(jnp.int32, rest.shape, 1)
             rest = jnp.where(jnp.logical_and(col_at >= tall * q, col_at < low), 0.0, rest)
-            work[low:BLK, :] = rest - outer(done[:, low:BLK], past)
+            work[low:BLK, :] = rest - dot_f32(done[:, low:BLK], past, ((0,), (0,)))
     lower = (
         lax.broadcasted_iota(jnp.int32, (BLK, BLK), 0)
         >= lax.broadcasted_iota(jnp.int32, (BLK, BLK), 1)

time: 99.2 us -> 98.2 us (0.990)
  Pallas kernels: 98.4 us -> 97.4 us
where the time goes in v5:
time: 98.2 us; the launch traced here: 98 us
  Pallas kernels  97.4 us (99%)
    pallas_call x1, Pallas kernels, gram_everywhere(): pl.pallas_call(functools.partial(gram_kernel, n_rows), out_shape=(jax.Sha...  83.5 us
    pallas_call x1, Pallas kernels, factor_and_solve(): pl.pallas_call(factor_kernel, out_shape=(jax.ShapeDtypeStruct((512, BLK),...  13.9 us

profile of v5, /device:TPU:1, one launch (start us, length us, event | category | flops | bytes accessed | tf_op | source)
XLA Modules:
  0.0 98.0 jit_solution(3412857435409765268)
XLA Ops:
  0.6 83.5 %gram.1 = (f32[2,2,3,64,128]{4,3,2,1,0:T(8,128)S(1)}, f32[2,3,2,64,128]{4,3,2,1,0:T(8,128)S(1)}, f32[4,128,128]{2,1,0:T(8,128)S(1)}) custom-call(bf16[8192,128]{1,0:T(8,128)(2,1)} %base_ref.1, f32[8,1024]{1,0:T(8,128)} %field_hbm.1, bf16[8,1024]{1,0:T(8,128)(2,1)} %grad_hbm.1, s32[1,128]{1,0:T(1,128)} %bitcast.3, s32[1,128]{1,0:T(1,128)} %bitcast.4), custom_call_target="tpu_custom_call" | custom-call | tf_op jit(solution)/shard_map/gram/pallas_call | solution.py:530
  84.1 13.9 %factor.1 = (f32[512,128]{1,0:T(8,128)}, f32[4,128]{1,0:T(4,128)}) custom-call(f32[2,2,3,64,128]{4,3,2,1,0:T(8,128)S(1)} %get-tuple-element.7.head_a, f32[2,3,2,64,128]{4,3,2,1,0:T(8,128)S(1)} %get-tuple-element.8.head_b, f32[4,128,128]{2,1,0:T(8,128)S(1)} %get-tuple-element.9.own_ref), custom_call_target="tpu_custom_call" | custom-call | tf_op jit(solution)/shard_map/factor/pallas_call | solution.py:696

commit v6 on v5

--- a/solution.py
+++ b/solution.py
@@ -19,6 +19,7 @@
 FIRST_Y = (0, 4, 8, 12)
 HALF = 14
 ROWS = BLK // 2
+LEAD = 48
 PARTS = 2
 
 
@@ -241,7 +242,6 @@
     cp.start()
     sent.append(cp)
     cp.wait_recv()
-    half[...] = parts[core] + from_core[...]
 
     def xa_copy(xx, d, peer):
         span = COUNT_X[xx]
@@ -257,11 +257,14 @@
             yb_send.at[d], yb_recv.at[d], dev_y(peer),
         )
 
+    half[0:HALF] = parts[core, 0:HALF] + from_core[0:HALF]
     for q in range(4):
         @pl.when(x != q)
         def _():
             xa_copy(q, (q + NX - x) % NX, q).start()
 
+    half[HALF:2 * HALF] = parts[core, HALF:2 * HALF] + from_core[HALF:2 * HALF]
+    for q in range(4):
         @pl.when(y != q)
         def _():
             yb_copy(q, (q + NY - y) % NY, q).start()
@@ -276,6 +279,22 @@
                 total = total + from_x[d, 0:span]
             sum_a[0:span] = total
 
+    skip = jnp.where(y == 3, 2, 0)
+    holds = jnp.logical_or(x >= 2, y < 3)
+
+    def ya_copy(d, yy, peer):
+        return remote(sum_a.at[yy], from_y2.at[d], ya_send.at[d], ya_recv.at[d], dev_y(peer))
+
+    def xb_copy(d, spot, peer):
+        return remote(sum_b.at[spot], from_x2.at[d], xb_send.at[d], xb_recv.at[d], dev_x(peer))
+
+    for d in range(1, 4):
+        yy = (y + d) % NY
+
+        @pl.when(jnp.logical_or(x >= 2, yy < 3))
+        def _():
+            ya_copy(d, yy, yy).start()
+
     for q in range(4):
         @pl.when(y == q)
         def _():
@@ -286,22 +305,8 @@
                 total = total + from_y[d, 0:span]
             sum_b[0:span] = total
 
-    skip = jnp.where(y == 3, 2, 0)
-    holds = jnp.logical_or(x >= 2, y < 3)
-
-    def ya_copy(d, yy, peer):
-        return remote(sum_a.at[yy], from_y2.at[d], ya_send.at[d], ya_recv.at[d], dev_y(peer))
-
-    def xb_copy(d, spot, peer):
-        return remote(sum_b.at[spot], from_x2.at[d], xb_send.at[d], xb_recv.at[d], dev_x(peer))
-
     for d in range(1, 4):
-        yy = (y + d) % NY
         xx = (x + d) % NX
-
-        @pl.when(jnp.logical_or(x >= 2, yy < 3))
-        def _():
-            ya_copy(d, yy, yy).start()
 
         @pl.when(jnp.logical_or(xx >= 2, y < 3))
         def _():
@@ -329,13 +334,13 @@
 
     def gy_head(d, spot, peer):
         return remote(
-            line.at[pl.ds(0, ROWS)], out_a.at[core, x, spot],
+            line.at[pl.ds(0, LEAD)], out_a.at[core, x, spot],
             gy_send.at[d], gy_recv.at[d], dev_y(peer),
         )
 
     def gx_head(d, spot, peer):
         return remote(
-            line.at[pl.ds(ROWS, ROWS)], out_b.at[core, y, spot],
+            line.at[pl.ds(LEAD, BLK - LEAD)], out_b.at[core, y, spot],
             gx_send.at[d], gx_recv.at[d], dev_x(peer),
         )
 
@@ -385,8 +390,8 @@
             for d in range(1, 4):
                 gy_head(d, y, (y + d) % NY).start()
                 gx_head(d, x, (x + d) % NX).start()
-            out_a[core, x, y] = line[0:ROWS]
-            out_b[core, y, x] = line[ROWS:BLK]
+            out_a[core, x, y] = line[0:LEAD]
+            out_b[core, y, x] = line[LEAD:BLK]
 
     def hx_copy(d, xx, peer):
         return remote(
@@ -530,8 +535,8 @@
     return pl.pallas_call(
         functools.partial(gram_kernel, n_rows),
         out_shape=(
-            jax.ShapeDtypeStruct((2, 2, 3, ROWS, BLK), f32),
-            jax.ShapeDtypeStruct((2, 3, 2, ROWS, BLK), f32),
+            jax.ShapeDtypeStruct((2, 2, 3, LEAD, BLK), f32),
+            jax.ShapeDtypeStruct((2, 3, 2, BLK - LEAD, BLK), f32),
             jax.ShapeDtypeStruct((4, BLK, BLK), f32),
         ),
         in_specs=[hbm] * 5,
@@ -647,8 +652,8 @@
     c = lax.axis_index("cols")
     for spot in range(12):
         k, at_x, at_y = spot // 6, spot // 3 % 2, spot % 3
-        head_ref[spot, 0:ROWS] = head_a[k, at_x, at_y]
-        head_ref[spot, ROWS:BLK] = head_b[k, at_y, at_x]
+        head_ref[spot, 0:LEAD] = head_a[k, at_x, at_y]
+        head_ref[spot, LEAD:BLK] = head_b[k, at_y, at_x]
     near = jnp.minimum(c, 3)
     for k in range(4):
         for j in range(k, 4):

time: 98.2 us -> 98.7 us (level)
  no operation moved by 1% of the time
where the time goes in v6:
time: 98.7 us; the launch traced here: 98.5 us
  Pallas kernels  97.9 us (99%)
    pallas_call x1, Pallas kernels, gram_everywhere(): pl.pallas_call(functools.partial(gram_kernel, n_rows), out_shape=(jax.Sha...  84 us
    pallas_call x1, Pallas kernels, factor_and_solve(): pl.pallas_call(factor_kernel, out_shape=(jax.ShapeDtypeStruct((512, BLK),...  13.9 us

profile of v6, /device:TPU:1, one launch (start us, length us, event | category | flops | bytes accessed | tf_op | source)
XLA Modules:
  0.0 98.5 jit_solution(12067423575491349382)
XLA Ops:
  0.6 84.0 %gram.1 = (f32[2,2,3,48,128]{4,3,2,1,0:T(8,128)S(1)}, f32[2,3,2,80,128]{4,3,2,1,0:T(8,128)S(1)}, f32[4,128,128]{2,1,0:T(8,128)S(1)}) custom-call(bf16[8192,128]{1,0:T(8,128)(2,1)} %base_ref.1, f32[8,1024]{1,0:T(8,128)} %field_hbm.1, bf16[8,1024]{1,0:T(8,128)(2,1)} %grad_hbm.1, s32[1,128]{1,0:T(1,128)} %bitcast.3, s32[1,128]{1,0:T(1,128)} %bitcast.4), custom_call_target="tpu_custom_call" | custom-call | tf_op jit(solution)/shard_map/gram/pallas_call | solution.py:535
  84.6 13.9 %factor.1 = (f32[512,128]{1,0:T(8,128)}, f32[4,128]{1,0:T(4,128)}) custom-call(f32[2,2,3,48,128]{4,3,2,1,0:T(8,128)S(1)} %get-tuple-element.7.head_a, f32[2,3,2,80,128]{4,3,2,1,0:T(8,128)S(1)} %get-tuple-element.8.head_b, f32[4,128,128]{2,1,0:T(8,128)S(1)} %get-tuple-element.9.own_ref), custom_call_target="tpu_custom_call" | custom-call | tf_op jit(solution)/shard_map/factor/pallas_call | solution.py:701

commit v7 on v6

--- a/solution.py
+++ b/solution.py
@@ -648,7 +648,7 @@
     inv[...] = jnp.where(lower, inv[...], 0.0)
 
 
-def factor_kernel(head_a, head_b, own_ref, r_ref, m_ref, mat, head_ref, work, inv):
+def factor_kernel(head_a, head_b, own_ref, r_ref, m_ref, mat, back, head_ref, work, inv):
     c = lax.axis_index("cols")
     for spot in range(12):
         k, at_x, at_y = spot // 6, spot // 3 % 2, spot % 3
@@ -687,12 +687,14 @@
             mat[i, :, i * BLK:768] = mat[i, :, i * BLK:768] - dot_f32(
                 mat[k, :, i * BLK:(i + 1) * BLK], mat[k, :, i * BLK:768], ((0,), (0,))
             )
-    rest = [mat[k, :, 640:768] for k in range(4)]
+        back[k, :, low:512] = dot_f32(inverse, mat[k, :, low:512], ((0,), (0,)))
+        back[k, :, 640:768] = dot_f32(inverse, mat[k, :, 640:768], ((0,), (0,)))
+    rest = [back[k, :, 640:768] for k in range(3)]
+    rest.append(dot_f32(inv[3], mat[3, :, 640:768], ((0,), (0,))))
     for k in (3, 2, 1, 0):
-        solved = dot_f32(inv[k], rest[k], ((0,), (0,)))
         for i in range(k):
-            rest[i] = rest[i] - dot_f32(mat[i, :, k * BLK:(k + 1) * BLK], solved)
-        m_ref[k:k + 1, :] = solved.T[0:1, :]
+            rest[i] = rest[i] - dot_f32(back[i, :, k * BLK:(k + 1) * BLK], rest[k])
+        m_ref[k:k + 1, :] = rest[k].T[0:1, :]
 
 
 def factor_and_solve(head_a, head_b, own):
@@ -708,6 +710,7 @@
         out_specs=(vmem, vmem),
         scratch_shapes=[
             pltpu.VMEM((4, BLK, 768), f32),
+            pltpu.VMEM((3, BLK, 768), f32),
             pltpu.VMEM((12, BLK, BLK), f32),
             pltpu.VMEM((BLK, BLK), f32),
             pltpu.VMEM((4, BLK, BLK), f32),

time: 98.7 us -> 98.2 us (level)
  no operation moved by 1% of the time
where the time goes in v7:
time: 98.2 us; the launch traced here: 98 us
  Pallas kernels  97.4 us (99%)
    pallas_call x1, Pallas kernels, gram_everywhere(): pl.pallas_call(functools.partial(gram_kernel, n_rows), out_shape=(jax.Sha...  84 us
    pallas_call x1, Pallas kernels, factor_and_solve(): pl.pallas_call(factor_kernel, out_shape=(jax.ShapeDtypeStruct((512, BLK),...  13.4 us

profile of v7, /device:TPU:1, one launch (start us, length us, event | category | flops | bytes accessed | tf_op | source)
XLA Modules:
  0.0 98.0 jit_solution(7693585934746620015)
XLA Ops:
  0.6 84.0 %gram.1 = (f32[2,2,3,48,128]{4,3,2,1,0:T(8,128)S(1)}, f32[2,3,2,80,128]{4,3,2,1,0:T(8,128)S(1)}, f32[4,128,128]{2,1,0:T(8,128)S(1)}) custom-call(bf16[8192,128]{1,0:T(8,128)(2,1)} %base_ref.1, f32[8,1024]{1,0:T(8,128)} %field_hbm.1, bf16[8,1024]{1,0:T(8,128)(2,1)} %grad_hbm.1, s32[1,128]{1,0:T(1,128)} %bitcast.3, s32[1,128]{1,0:T(1,128)} %bitcast.4), custom_call_target="tpu_custom_call" | custom-call | tf_op jit(solution)/shard_map/gram/pallas_call | solution.py:535
  84.6 13.4 %factor.1 = (f32[512,128]{1,0:T(8,128)}, f32[4,128]{1,0:T(4,128)}) custom-call(f32[2,2,3,48,128]{4,3,2,1,0:T(8,128)S(1)} %get-tuple-element.7.head_a, f32[2,3,2,80,128]{4,3,2,1,0:T(8,128)S(1)} %get-tuple-element.8.head_b, f32[4,128,128]{2,1,0:T(8,128)S(1)} %get-tuple-element.9.own_ref), custom_call_target="tpu_custom_call" | custom-call | tf_op jit(solution)/shard_map/factor/pallas_call | solution.py:703
